TPU v7x, 256 devices: a whole 4x4x8 slice. The times are simulated.
256 devices in a mesh: ctx: 4 (over y_lo, core), exp: 64 (over z, x, y_hi).
Axes of the slice: x: 4, y: 4 (y_hi: 2, y_lo: 2; y = y_hi * 2 + y_lo), z: 8, core: 2. Of those that a mesh axis runs over, the one named last changes fastest.
Arguments:
- residual_in: bfloat16 [2048, 3584], P(('ctx', 'exp')), may hold values from -1.5 to 1.5
- norm_gain: float32 [3584], replicated, may hold values from 0.25 to 1.75
- q_nope: bfloat16 [2048, 128, 512], P('ctx', 'exp'), may hold values from -64 to 64
- q_rope: bfloat16 [2048, 8192], P('ctx', 'exp'), may hold values from -6 to 6
- latent: bfloat16 [2048, 512], P('ctx'), may hold values from -6 to 6
- k_rope: bfloat16 [2048, 64], P('ctx'), may hold values from -6 to 6
- doc_ids: int32 [2048], P('ctx'), may hold values from 0 to 3, never falling along the last dimension, each value on 1 to 1024 neighbouring positions
- uv_weight: bfloat16 [128, 512, 128], P('exp'), may hold values from -0.25 to 0.25
- out_weight: bfloat16 [16384, 3584], P('exp'), may hold values from -0.046875 to 0.046875
- expert_ids: int32 [2048, 8], P(('ctx', 'exp')), may hold values from 0 to 63, all different within a row; in each aligned block of 8 rows (0 to 7, 8 to 15, ...) at most 2 rows name the same one
- gate_levels: int32 [2048, 8], P(('ctx', 'exp')), may hold values from 1 to 255
- bin_ids: int32 [2048, 8], P(('ctx', 'exp')), may hold values from 0 to 2047
- gate_weight: bfloat16 [64, 3584, 1024], P('exp', None, 'ctx'), may hold values from -0.09375 to 0.09375
- up_weight: bfloat16 [64, 3584, 1024], P('exp', None, 'ctx'), may hold values from -0.09375 to 0.09375
- down_weight: bfloat16 [64, 1024, 3584], P('exp', 'ctx'), may hold values from -0.1875 to 0.1875
Outputs:
- layer_out: bfloat16 [2048, 3584], P(('ctx', 'exp'))
- histogram: float32 [64, 2048], P('exp', 'ctx')
Inputs may be any that keep to these rules, and one draw needn't show every extreme that they name: `expert_ids`: each row names 8 different experts; within the rows of one device (aligned blocks of 8 rows) no expert is named more than 2 times, a bound that some block reaches. `doc_ids`: document numbers never fall along the sequence; each document has 1 to 1024 tokens, one exactly 1024.
All inputs are finite; a program needn't handle non-finite values.
Results may differ from a plain program's by a relative error of at most 0.03.
Values may be sent and summed in bfloat16 or wider, within the bound.
A program may use at most 128 MiB of HBM per device.

v0:
```python
import jax
import jax.numpy as jnp
from jax import lax
from jax.sharding import PartitionSpec as P

HID = 1024
NBINS = 2048


softmax_scale = 192.0 ** (-0.5)
norm_eps = 1e-06
masked_score = -1e30


def route_slots(expert_ids, experts, capacity):
    flat_ids = expert_ids.reshape(-1)
    onehot = (flat_ids[:, None] == jnp.arange(experts, dtype=jnp.int32)[None, :]).astype(jnp.int32)
    before = jnp.cumsum(onehot, axis=0) - onehot
    slot_rank = jnp.sum(before * onehot, axis=1)
    return (flat_ids * capacity + slot_rank).reshape(expert_ids.shape)


def key_scores(query_nope, query_rope, lat_rows, rope_rows):
    scores = jnp.einsum("qhl,kl->hqk", query_nope, lat_rows, preferred_element_type=jnp.float32)
    scores = scores + jnp.einsum(
        "qhr,kr->hqk", query_rope, rope_rows, preferred_element_type=jnp.float32
    )
    return scores * softmax_scale


def attend_piece(running, key_piece, query_nope, query_rope, query_pos, query_docs):
    lat_rows, rope_rows, doc_rows = key_piece
    key_pos = jnp.arange(lat_rows.shape[0], dtype=jnp.int32)
    allowed = (key_pos[None, :] <= query_pos[:, None]) & (doc_rows[None, :] == query_docs[:, None])
    scores = jnp.where(
        allowed[None], key_scores(query_nope, query_rope, lat_rows, rope_rows), masked_score
    )
    run_max, run_sum, accum = running
    new_max = jnp.maximum(run_max, jnp.max(scores, axis=2))
    probs = jnp.where(allowed[None], jnp.exp(scores - new_max[:, :, None]), 0.0)
    run_sum = jnp.sum(probs, axis=2)
    accum = jnp.einsum(
        "hqk,kl->hql", probs.astype(jnp.bfloat16), lat_rows, preferred_element_type=jnp.float32
    )
    return (new_max, run_sum, accum)


def project_values(context, uv_weight):
    values = jnp.einsum(
        "hql,hlv->qhv", context, uv_weight, preferred_element_type=jnp.float32
    ).astype(jnp.bfloat16)
    return values.reshape(values.shape[0], values.shape[1] * values.shape[2])


def fold_projection(running, uv_weight, out_weight):
    context = (running[2] / running[1][:, :, None]).astype(jnp.bfloat16)
    values = project_values(context, uv_weight)

    def head_rows(row_start, row_count):
        return jnp.dot(values, out_weight, preferred_element_type=jnp.float32)

    return head_rows


def expert_hidden(row_data, w_gate, w_up):
    gate_part = jnp.dot(row_data, w_gate, preferred_element_type=jnp.float32)
    up_part = jnp.dot(row_data, w_up, preferred_element_type=jnp.float32)
    activation = jax.nn.silu(gate_part) * up_part
    return (activation.astype(jnp.bfloat16), jnp.sum(activation * activation, axis=1) / HID)


def bin_energy(energy, slot_bins):
    onehot = (slot_bins[:, None] == jnp.arange(NBINS, dtype=jnp.int32)[None, :]).astype(jnp.float32)
    return jnp.dot(energy[None, :], onehot, precision=lax.Precision.HIGHEST)[0]


def on_device(
    residual_in,
    norm_gain,
    q_nope,
    q_rope,
    latent,
    k_rope,
    doc_ids,
    uv_weight,
    out_weight,
    expert_ids,
    gate_levels,
    bin_ids,
    gate_weight,
    up_weight,
    down_weight,
):
    exp_devices = lax.axis_size("exp")
    block_len, head_count, lat_width = q_nope.shape
    rope_width = k_rope.shape[1]
    query_first = lax.axis_index("ctx") * block_len
    query_pos = query_first + jnp.arange(block_len, dtype=jnp.int32)
    query_rope = q_rope.reshape(block_len, head_count, rope_width)
    token_count = residual_in.shape[0]
    keys_local = (latent, k_rope, doc_ids)
    initial = (
        jnp.full((head_count, block_len), masked_score, jnp.float32),
        jnp.zeros((head_count, block_len), jnp.float32),
        jnp.zeros((head_count, block_len, lat_width), jnp.float32),
    )
    running = attend_piece(
        initial,
        (
            lax.all_gather(keys_local[0], "ctx", axis=0, tiled=True),
            lax.all_gather(keys_local[1], "ctx", axis=0, tiled=True),
            lax.all_gather(keys_local[2], "ctx", axis=0, tiled=True),
        ),
        q_nope,
        query_rope,
        query_pos,
        doc_ids,
    )
    head_rows = fold_projection(running, uv_weight, out_weight)
    attended = lax.psum_scatter(
        head_rows(jnp.int32(0), token_count * lax.axis_size("exp")),
        "exp",
        scatter_dimension=0,
        tiled=True,
    )
    stream_state = residual_in.astype(jnp.float32) + attended
    normed = (
        stream_state
        * lax.rsqrt(jnp.mean(stream_state * stream_state, axis=1, keepdims=True) + norm_eps)
        * norm_gain
    ).astype(jnp.bfloat16)
    top_count = expert_ids.shape[1]
    capacity = min(token_count, max(2, 2 * token_count * top_count // exp_devices))
    slot_total = exp_devices * capacity
    destination = route_slots(expert_ids, exp_devices, capacity)
    slot_match = destination[:, :, None] == jnp.arange(slot_total, dtype=jnp.int32)[None, None, :]
    selector = jnp.sum(slot_match.astype(jnp.int32), axis=1).astype(jnp.bfloat16)
    outgoing = jnp.einsum("ts,td->sd", selector, normed, preferred_element_type=jnp.float32).astype(
        jnp.bfloat16
    )
    outgoing = outgoing.reshape(exp_devices, capacity, outgoing.shape[1])
    slot_bins = jnp.sum(jnp.where(slot_match, bin_ids[:, :, None], 0), axis=(0, 1)).reshape(
        exp_devices, capacity
    )
    incoming, incoming_bins = (
        lax.all_to_all(outgoing, "exp", split_axis=0, concat_axis=1, tiled=True),
        lax.all_to_all(slot_bins, "exp", split_axis=0, concat_axis=1, tiled=True),
    )
    all_rows, all_bins = (
        lax.all_gather(incoming, "ctx", axis=1, tiled=True),
        lax.all_gather(incoming_bins, "ctx", axis=1, tiled=True),
    )
    hidden, energy = expert_hidden(all_rows[0], gate_weight[0], up_weight[0])
    bin_part = bin_energy(energy, all_bins[0])
    down_local = down_weight[0]
    expert_out = lax.psum_scatter(
        jnp.dot(hidden, down_local, preferred_element_type=jnp.float32).astype(jnp.bfloat16),
        "ctx",
        scatter_dimension=0,
        tiled=True,
    )
    histogram = lax.psum_scatter(bin_part[None, :], "ctx", scatter_dimension=1, tiled=True)
    returned = lax.all_to_all(expert_out[None], "exp", split_axis=1, concat_axis=0, tiled=True)
    levels = gate_levels.astype(jnp.float32)
    route_weights = levels / jnp.sum(levels, axis=1, keepdims=True)
    combiner = jnp.sum(jnp.where(slot_match, route_weights[:, :, None], 0.0), axis=1)
    mixture = jnp.dot(
        combiner,
        returned.reshape(slot_total, returned.shape[2]).astype(jnp.float32),
        precision=lax.Precision.HIGHEST,
    )
    layer_out = (stream_state + mixture).astype(jnp.bfloat16)
    return (layer_out, histogram)


def solution(mesh):
    return jax.shard_map(
        on_device,
        mesh=mesh,
        in_specs=(
            P(("ctx", "exp"), None),
            P(),
            P("ctx", "exp", None),
            P("ctx", "exp"),
            P("ctx", None),
            P("ctx", None),
            P("ctx"),
            P("exp", None, None),
            P("exp", None),
            P(("ctx", "exp"), None),
            P(("ctx", "exp"), None),
            P(("ctx", "exp"), None),
            P("exp", None, "ctx"),
            P("exp", None, "ctx"),
            P("exp", "ctx", None),
        ),
        out_specs=(P(("ctx", "exp"), None), P("exp", "ctx")),
        check_vma=False,
    )
```

profile of v0, /device:TPU:1, one launch (start us, length us, event | category | flops | bytes accessed | tf_op | source)
XLA Modules:
  0.0 649.6 jit_solution(16542535418306436158)
XLA Ops:
  7.2 0.0 copy-start
  7.2 0.0 all-gather.4.cloned.1.call-start
  7.2 0.7 all-gather.4.cloned.1.call-update
  7.9 0.0 reduce-scatter.6.cloned.1.call-start
  8.0 1.0 copy.36
  9.0 8.3 %all-gather = s32[4,1,512]{2,1,0:T(1,128)S(1)} all-gather(s32[1,1,512]{2,1,0:T(1,128)} %bitcast.73), channel_id=1, replica_groups=mesh['ctx'=4,'exp'=64] {'ctx'}, dimensions={0}, use_global_device_ids=true | all-gather | bytes 10240 | tf_op jit(solution)/shard_map/all_gather | solution.py:112
  17.3 6.1 all_gather.17
  23.4 1.7 fusion.7
  25.1 20.7 %all-gather.4.cloned.1.call-done = bf16[2048,512]{1,0:T(8,128)(2,1)} async-done(((bf16[512,512]{1,0:T(8,128)(2,1)}), bf16[2048,512]{1,0:T(8,128)(2,1)}) %all-gather.4.cloned.1.call-update) | async-done | bytes 2097168 | tf_op jit(solution)/shard_map/all_gather | solution.py:110
  45.7 4.2 fusion.16
  50.0 2.3 fusion.46
  52.3 3.2 copy-done.1
  55.5 1.7 fusion
  57.2 6.8 %convolution_convert_fusion.2 = bf16[2,512,128]{1,2,0:T(8,128)(2,1)S(1)} fusion(bf16[2,512,128]{2,1,0:T(8,128)(2,1)S(1)} %copy-done.11, f32[2,512]{1,0:T(2,128)S(1)} %fusion, f32[2,512,2048]{1,2,0:T(8,128)} %copy-done.1, f32[2,512]{1,0:T(2,128)S(1)} %broadcast_maximum_fusion, pred[512,2048]{0,1:T(8,128)(4,1)S(1)} %fusion.7, ...), kind=kOutput, calls=%fused_computation.30 | convolution fusion | flops 2289172480 | bytes 12066816 | tf_op jit(solution)/shard_map/hql,hlv->qhv/dot_general | solution.py:49
  64.0 4.1 fusion.47
  68.1 0.0 reduce-scatter.6.cloned.1.call-update
  68.2 0.2 all-gather.6.cloned.1.call-start
  68.4 0.4 copy-done.6
  68.8 0.1 eq.61
  68.9 0.1 fusion.42
  69.0 0.1 reduce_window_sum.11
  69.1 0.2 select_reduce_fusion.2
  69.3 0.1 reduce_sum.76
  69.3 0.0 copy-done.8
  69.4 0.1 select_reduce_fusion
  69.5 327.8 %reduce-scatter.6.cloned.1.call-done = f32[8,3584]{1,0:T(8,128)} async-done(((f32[512,3584]{1,0:T(8,128)}), f32[8,3584]{1,0:T(8,128)}) %reduce-scatter.6.cloned.1.call-update) | async-done | bytes 114704 | tf_op jit(solution)/shard_map/reduce_scatter | solution.py:120
  397.2 1.0 multiply_reduce_fusion.1
  398.3 2.3 convolution_convert_fusion.1
  400.6 2.3 reshape.112
  402.9 24.6 %all_to_all.37 = bf16[64,2,3584]{2,1,0:T(2,128)(2,1)} all-to-all(bf16[64,2,3584]{2,1,0:T(2,128)(2,1)S(1)} %reshape.112), channel_id=1, replica_groups=mesh['ctx'=4,'exp'=64] {'exp'}, dimensions={0} | all-to-all | bytes 1835008 | tf_op jit(solution)/shard_map/all_to_all | solution.py:146
  427.5 3.2 all_to_all.14
  430.7 0.0 all-gather.6.cloned.1.call-update
  430.7 0.0 reduce-scatter.8.cloned.1.call-start
  430.8 91.2 %all-gather.6.cloned.1.call-done = bf16[1,512,3584]{2,1,0:T(8,128)(2,1)} async-done(((bf16[1,128,3584]{2,1,0:T(8,128)(2,1)}), bf16[1,512,3584]{2,1,0:T(8,128)(2,1)}) %all-gather.6.cloned.1.call-update) | async-done | bytes 3670032 | tf_op jit(solution)/shard_map/all_gather | solution.py:150
  522.0 3.9 fusion.12
  525.9 0.3 copy-done.10
  526.2 1.2 multiply_reduce_fusion
  527.5 0.3 copy-done.2
  527.7 2.9 convolution_convert_fusion
  530.7 0.0 reduce-scatter.8.cloned.1.call-update
  530.7 0.8 all_to_all.31
  531.5 12.5 %all-to-all-start.2 = ((s32[64,1,2]{2,1,0:T(1,128)}), s32[64,1,2]{2,1,0:T(1,128)S(1)}, u32[]{:S(2)}, u32[]{:S(2)}) async-start(s32[64,1,2]{2,1,0:T(1,128)} %bitcast.14), calls=%async_computation.4 | async-start | bytes 65536 | tf_op jit(solution)/shard_map/all_to_all | solution.py:147
  544.0 31.6 %reduce-scatter.8.cloned.1.call-done = bf16[128,3584]{1,0:T(8,128)(2,1)} async-done(((bf16[512,3584]{1,0:T(8,128)(2,1)}), bf16[128,3584]{1,0:T(8,128)(2,1)}) %reduce-scatter.8.cloned.1.call-update) | async-done | bytes 917520 | tf_op jit(solution)/shard_map/reduce_scatter | solution.py:156
  575.6 3.8 copy.53
  579.4 0.5 broadcast.82
  580.0 7.2 %reduce.4 = bf16[128,3584]{1,0:T(8,128)(2,1)S(1)} reduce(bf16[128,1,3584]{2,1,0:T(2,128)(2,1)} %bitcast.66, bf16[]{:T(256)} %broadcast.82), dimensions={1}, to_apply=%bitcast.65.reduce_sub_computation | reduce | bytes 1835010
  587.2 1.3 reshape.131
  588.5 0.0 all-to-all-done.2
  588.5 12.4 %all-to-all-start.1 = ((bf16[64,2,3584]{2,1,0:T(2,128)(2,1)}), bf16[64,2,3584]{2,1,0:T(2,128)(2,1)S(1)}, u32[]{:S(2)}, u32[]{:S(2)}) async-start(bf16[64,2,3584]{2,1,0:T(2,128)(2,1)} %reshape.131), calls=%async_computation.3 | async-start | bytes 1835008 | tf_op jit(solution)/shard_map/all_to_all | solution.py:163
  600.9 0.0 reduce-scatter.10.cloned.1.call-start
  601.0 0.1 convert_reduce_fusion.1
  601.1 0.1 convert_divide_fusion
  601.2 0.5 broadcast.81
  601.7 0.7 reduce.3
  602.4 0.1 all_to_all.33
  602.6 5.8 all_gather.19
  608.4 4.5 fusion.14
  612.9 0.0 reduce-scatter.10.cloned.1.call-update
  612.9 0.1 select_reduce_fusion.1
  613.0 23.8 %reduce-scatter.10.cloned.1.call-done = f32[512,1]{1,0:T(8,128)} async-done(((f32[2048,1]{1,0:T(8,128)}), f32[512,1]{1,0:T(8,128)}) %reduce-scatter.10.cloned.1.call-update) | async-done | bytes 2064
  636.7 1.6 copy.44
  638.4 0.0 all-to-all-done.1
  638.4 2.1 reshape.132
  640.5 2.6 fusion.2
  (23 shorter events, 0.1 us)
Async XLA Ops:
  7.2 56.8 %copy-start = (bf16[256,3584]{1,0:T(8,128)(2,1)S(1)}, bf16[256,3584]{1,0:T(8,128)(2,1)}, u32[]{:S(2)}) copy-start(bf16[256,3584]{1,0:T(8,128)(2,1)} %param.23) | copy-start | bytes 5505028
  7.2 38.6 %all-gather.4.cloned.1.call-start = ((), (), s32[]{:S(2)}) async-start(), calls=%async_computation.6 | async-start | bytes 2621440 | tf_op jit(solution)/shard_map/all_gather | solution.py:110
  7.9 389.3 %reduce-scatter.6.cloned.1.call-start = ((), (), s32[]{:S(2)}) async-start(), calls=%async_computation.7 | async-start | bytes 7454720 | tf_op jit(solution)/shard_map/reduce_scatter | solution.py:120
  52.3 3.2 copy-start.1
  55.5 1.7 copy-start.11
  68.1 0.7 copy-start.6
  68.1 1.2 copy-start.8
  68.1 329.1 %copy-start.4 = (bf16[8,3584]{1,0:T(8,128)(2,1)S(1)}, bf16[8,3584]{1,0:T(8,128)(2,1)}, u32[]{:S(2)}) copy-start(bf16[8,3584]{1,0:T(8,128)(2,1)} %param.15) | copy-start | bytes 172036
  68.1 330.2 %copy-start.5 = (f32[3584]{0:T(1024)S(1)}, f32[3584]{0:T(1024)}, u32[]{:S(2)}) copy-start(f32[3584]{0:T(1024)} %param.16) | copy-start | bytes 43012
  68.2 453.8 %all-gather.6.cloned.1.call-start = ((), (), s32[]{:S(2)}) async-start(), calls=%async_computation.8 | async-start | bytes 4587520 | tf_op jit(solution)/shard_map/all_gather | solution.py:150
  430.7 144.9 %reduce-scatter.8.cloned.1.call-start = ((), (), s32[]{:S(2)}) async-start(), calls=%async_computation.9 | async-start | bytes 4587520 | tf_op jit(solution)/shard_map/reduce_scatter | solution.py:156
  522.0 3.9 copy-start.9
  522.0 4.3 copy-start.10
  526.2 1.5 copy-start.2
  531.5 57.0 %all-to-all-start.2 = ((s32[64,1,2]{2,1,0:T(1,128)}), s32[64,1,2]{2,1,0:T(1,128)S(1)}, u32[]{:S(2)}, u32[]{:S(2)}) async-start(s32[64,1,2]{2,1,0:T(1,128)} %bitcast.14), calls=%async_computation.4 | async-start | bytes 65536 | tf_op jit(solution)/shard_map/all_to_all | solution.py:147
  579.4 21.6 %copy-start.7 = (s32[8,8]{1,0:T(8,128)S(1)}, s32[8,8]{1,0:T(8,128)}, u32[]{:S(2)}) copy-start(s32[8,8]{1,0:T(8,128)} %param.25) | copy-start | bytes 772
  588.5 52.0 %copy-start.3 = (f32[8,3584]{1,0:T(8,128)S(1)}, f32[8,3584]{1,0:T(8,128)}, u32[]{:S(2)}) copy-start(f32[8,3584]{1,0:T(8,128)} %reduce-scatter.6.cloned.1.call-done) | copy-start | bytes 344068
  588.5 49.9 %all-to-all-start.1 = ((bf16[64,2,3584]{2,1,0:T(2,128)(2,1)}), bf16[64,2,3584]{2,1,0:T(2,128)(2,1)S(1)}, u32[]{:S(2)}, u32[]{:S(2)}) async-start(bf16[64,2,3584]{2,1,0:T(2,128)(2,1)} %reshape.131), calls=%async_computation.3 | async-start | bytes 1835008 | tf_op jit(solution)/shard_map/all_to_all | solution.py:163
  600.9 35.8 %reduce-scatter.10.cloned.1.call-start = ((), (), s32[]{:S(2)}) async-start(), calls=%async_computation.10 | async-start | bytes 1310720
Sparse Core Ops, SparseCore 0:
  9.8 35.8 all-gather.3
  68.3 328.9 reduce-scatter.5
  430.9 91.0 all-gather.5
  530.8 44.7 reduce-scatter.7
  613.0 23.6 reduce-scatter.9
where the time goes:
time: 650 us
  waiting for transfers between devices  496 us (76%)
  blocking collectives  44.8 us (7%)
  matrix products  34.9 us (5%)
  starting transfers between devices  25.4 us (4%)
  local copies, waits for them, and re-layouts  21.8 us (3%)
  between operations  14 us (2%)
  other arithmetic  13.1 us (2%)
    reduce_scatter x1, waiting for transfers between devices, on_device(): lax.psum_scatter(head_rows(jnp.int32(0), token_count * lax.axis_size('exp...  328 us
    all_gather x1, waiting for transfers between devices, on_device(): lax.all_gather(incoming, 'ctx', axis=1, tiled=True)  91.2 us
    reduce_scatter x1, waiting for transfers between devices, on_device(): lax.psum_scatter(jnp.dot(hidden, down_local, preferred_element_type=jnp.f...  31.6 us
    all_to_all x1, blocking collectives, on_device(): lax.all_to_all(outgoing, 'exp', split_axis=0, concat_axis=1, tiled=True)  24.6 us
    unnamed x6, waiting for transfers between devices  24.5 us
    all_gather x1, waiting for transfers between devices, on_device(): lax.all_gather(keys_local[0], 'ctx', axis=0, tiled=True)  20.7 us
  transfers between devices with their start and end apart: 7, of which 5 were waited for; matrix products, arithmetic and copies ran while one was open for 4% of the time, Pallas kernels for 0%

commit v1 on v0

v1 whole, which is shorter than its diff:
```python
import functools

import jax
import jax.numpy as jnp
from jax import lax
from jax.experimental import pallas as pl
from jax.experimental.pallas import tpu as pltpu
from jax.sharding import PartitionSpec as P

HID = 1024
NBINS = 2048


softmax_scale = 192.0 ** (-0.5)
norm_eps = 1e-06
masked_score = -1e30

NZ, NX, NY = 8, 4, 2
NQ = NX * NY
NR = NZ * NY
TOK = 8
CAP = 2
N_CTX = 4
N_EXPERTS = 64
MESH = pl.DeviceIdType.MESH


def remote(src, dst, send_sem, recv_sem, target):
    copy = pltpu.make_async_remote_copy(
        src_ref=src,
        dst_ref=dst,
        send_sem=send_sem,
        recv_sem=recv_sem,
        device_id=target,
        device_id_type=MESH,
    )
    copy.start()
    return copy


def greet(targets):
    barrier = pltpu.get_barrier_semaphore()
    for target in targets:
        pl.semaphore_signal(barrier, inc=1, device_id=target, device_id_type=MESH)
    pl.semaphore_wait(barrier, len(targets))


def project_sum_kernel(
    part_a,
    values_ref,
    weight_ref,
    out_ref,
    a_first,
    a_slots,
    b_first,
    b_slots,
    a_push,
    a_got,
    b_push,
    b_got,
    a_send_sem,
    a_recv_sem,
    b_send_sem,
    b_recv_sem,
    ap_send_sem,
    ap_recv_sem,
    bp_send_sem,
    bp_recv_sem,
):
    width = weight_ref.shape[1]
    half_a, half_b = part_a // 2, (width - part_a) // 2
    me = lax.axis_index("exp")
    z, x, y = me // NQ, (me // NY) % NX, me % NY
    q, r = x * NY + y, z * NY + y

    def at(z_at, x_at, y_at):
        return {"exp": (z_at * NX + x_at) * NY + y_at}

    q_peers = [(q + j) % NQ for j in range(NQ)]
    r_peers = [(r + j) % NR for j in range(NR)]
    z_next = [at((z + 1) % NZ, x, y), at((z + NZ - 1) % NZ, x, y)]
    x_next = [at(z, (x + 1) % NX, y), at(z, (x + NX - 1) % NX, y)]
    greet(
        [at(z, p // NY, p % NY) for p in q_peers[1:]]
        + [at(p // NY, x, p % NY) for p in r_peers[1:]]
    )

    def a_own(way, chunk):
        rows = values_ref[chunk].reshape(NX * NY * TOK, values_ref.shape[3])
        return jnp.dot(
            rows,
            weight_ref[:, way * half_a : (way + 1) * half_a],
            preferred_element_type=jnp.float32,
        )

    def b_own(way, chunk):
        rows = values_ref[:, chunk].reshape(NZ * NY * TOK, values_ref.shape[3])
        return jnp.dot(
            rows,
            weight_ref[:, part_a + way * half_b : part_a + (way + 1) * half_b],
            preferred_element_type=jnp.float32,
        )

    a_flight, b_flight, pushes = {}, {}, []

    def a_step(step):
        for way in range(2):
            sign = -1 if way == 0 else 1
            own = a_own(way, (z + sign * (1 + step) + 2 * NZ) % NZ)
            if step == 0:
                src = a_first.at[way]
                a_first[way] = own.astype(jnp.bfloat16)
            else:
                src = a_slots.at[way, step - 1]
                a_flight[way, step - 1].wait_recv()
                a_slots[way, step - 1] = (
                    a_slots[way, step - 1].astype(jnp.float32) + own
                ).astype(jnp.bfloat16)
            a_flight[way, step] = remote(
                src,
                a_slots.at[way, step],
                a_send_sem.at[way, step],
                a_recv_sem.at[way, step],
                z_next[way],
            )

    def b_step(step):
        for way in range(2):
            sign = -1 if way == 0 else 1
            own = b_own(way, (x + sign * (1 + step) + 2 * NX) % NX)
            if step == 0:
                src = b_first.at[way]
                b_first[way] = own.astype(jnp.bfloat16)
            else:
                src = b_slots.at[way, step - 1]
                b_flight[way, step - 1].wait_recv()
                b_slots[way, step - 1] = (
                    b_slots[way, step - 1].astype(jnp.float32) + own
                ).astype(jnp.bfloat16)
            b_flight[way, step] = remote(
                src,
                b_slots.at[way, step],
                b_send_sem.at[way, step],
                b_recv_sem.at[way, step],
                x_next[way],
            )

    def a_push_out():
        for way in range(2):
            own = a_own(way, z)
            a_flight[way, NZ - 2].wait_recv()
            own = own + a_slots[way, NZ - 2].astype(jnp.float32)
            a_push[:, :, way * half_a : (way + 1) * half_a] = own.reshape(
                NQ, TOK, half_a
            ).astype(jnp.bfloat16)
        for j in range(1, NQ):
            p = q_peers[j]
            pushes.append(
                remote(
                    a_push.at[p],
                    a_got.at[j - 1],
                    ap_send_sem.at[j - 1],
                    ap_recv_sem.at[j - 1],
                    at(z, p // NY, p % NY),
                )
            )

    def b_push_out():
        for way in range(2):
            own = b_own(way, x)
            b_flight[way, NX - 2].wait_recv()
            own = own + b_slots[way, NX - 2].astype(jnp.float32)
            b_push[:, :, way * half_b : (way + 1) * half_b] = own.reshape(
                NR, TOK, half_b
            ).astype(jnp.bfloat16)
        for j in range(1, NR):
            p = r_peers[j]
            pushes.append(
                remote(
                    b_push.at[p],
                    b_got.at[j - 1],
                    bp_send_sem.at[j - 1],
                    bp_recv_sem.at[j - 1],
                    at(p // NY, x, p % NY),
                )
            )

    a_step(0)
    b_step(0)
    a_step(1)
    a_step(2)
    b_step(1)
    a_step(3)
    b_step(2)
    a_step(4)
    b_push_out()
    a_step(5)
    a_step(6)
    a_push_out()
    for copy in pushes:
        copy.wait_recv()
    total = b_push[r].astype(jnp.float32)
    for j in range(NR - 1):
        total = total + b_got[j].astype(jnp.float32)
    out_ref[:, part_a:] = total
    total = a_push[q].astype(jnp.float32)
    for j in range(NQ - 1):
        total = total + a_got[j].astype(jnp.float32)
    out_ref[:, :part_a] = total
    for copy in [*a_flight.values(), *b_flight.values(), *pushes]:
        copy.wait_send()


def project_sum(values, weight, part_a=2048):
    rows, depth = values.shape
    width = weight.shape[1]
    part_b = width - part_a
    bf16 = jnp.bfloat16
    dma = pltpu.SemaphoreType.DMA
    return pl.pallas_call(
        functools.partial(project_sum_kernel, part_a),
        out_shape=jax.ShapeDtypeStruct((TOK, width), jnp.float32),
        in_specs=[pl.BlockSpec(memory_space=pltpu.VMEM)] * 2,
        out_specs=pl.BlockSpec(memory_space=pltpu.VMEM),
        scratch_shapes=[
            pltpu.VMEM((2, NQ * TOK, part_a // 2), bf16),
            pltpu.VMEM((2, NZ - 1, NQ * TOK, part_a // 2), bf16),
            pltpu.VMEM((2, NR * TOK, part_b // 2), bf16),
            pltpu.VMEM((2, NX - 1, NR * TOK, part_b // 2), bf16),
            pltpu.VMEM((NQ, TOK, part_a), bf16),
            pltpu.VMEM((NQ - 1, TOK, part_a), bf16),
            pltpu.VMEM((NR, TOK, part_b), bf16),
            pltpu.VMEM((NR - 1, TOK, part_b), bf16),
            dma((2, NZ - 1)),
            dma((2, NZ - 1)),
            dma((2, NX - 1)),
            dma((2, NX - 1)),
            dma((NQ - 1,)),
            dma((NQ - 1,)),
            dma((NR - 1,)),
            dma((NR - 1,)),
        ],
        compiler_params=pltpu.CompilerParams(
            collective_id=0, has_side_effects=True, vmem_limit_bytes=40 << 20
        ),
        name="project_sum",
    )(values.reshape(NZ, NX, NY * TOK, depth), weight)


def small(cond):
    return cond.astype(jnp.float32).astype(jnp.bfloat16)


def split3(v):
    first = v.astype(jnp.bfloat16)
    rest = v - first.astype(jnp.float32)
    second = rest.astype(jnp.bfloat16)
    third = (rest - second.astype(jnp.float32)).astype(jnp.bfloat16)
    return first, second, third


def mm(a, b):
    return jnp.dot(a, b, preferred_element_type=jnp.float32)


def mm_t(a, b):
    return lax.dot_general(
        a, b, (((0,), (0,)), ((), ())), preferred_element_type=jnp.float32
    )


def experts_kernel(
    rows_ref,
    state_ref,
    scale_ref,
    gate_hbm,
    up_hbm,
    down_hbm,
    out_ref,
    hist_ref,
    gate_ref,
    up_ref,
    down_ref,
    near,
    weigh,
    slots,
    inbox,
    kept,
    to_mate,
    from_mate,
    back,
    returned,
    to_y,
    from_y,
    to_z,
    from_z,
    hist_out,
    hist_in,
    load_sem,
    z_send,
    z_recv,
    y_send,
    y_recv,
    q_send,
    q_recv,
    m_send,
    m_recv,
    o_send,
    o_recv,
    b_send,
    b_recv,
    ys_send,
    ys_recv,
    zs_send,
    zs_recv,
    h_send,
    h_recv,
):
    width = state_ref.shape[1]
    sent = width + 2 * N_EXPERTS
    half_rows, half_slots = NZ * TOK, NQ * NZ * CAP
    piece = NZ * CAP
    ctx, me = lax.axis_index("ctx"), lax.axis_index("exp")
    y_lo, core = ctx // 2, ctx % 2
    z, q = me // NQ, me % NQ

    def z_peer(z_at):
        return {"ctx": ctx, "exp": z_at * NQ + q}

    def q_peer(q_at):
        return {"ctx": ctx, "exp": z * NQ + q_at}

    y_peer = {"ctx": (1 - y_lo) * 2 + core, "exp": me}
    mate = {"ctx": y_lo * 2 + 1 - core, "exp": me}

    def c_peer(j):
        return {"ctx": (ctx + j) % N_CTX, "exp": me}

    loads = [
        pltpu.make_async_copy(src, dst, load_sem.at[i])
        for i, (src, dst) in enumerate(
            ((gate_hbm, gate_ref), (up_hbm, up_ref), (down_hbm, down_ref))
        )
    ]
    for load in loads:
        load.start()
    greet(
        [z_peer((z + j) % NZ) for j in range(1, NZ)]
        + [q_peer((q + j) % NQ) for j in range(1, NQ)]
        + [c_peer(j) for j in range(1, N_CTX)]
    )
    pending = []

    order = (1, 7, 2, 6, 3, 5, 4)
    arrivals = {}
    for j in order:
        arrivals[j] = remote(
            rows_ref, near.at[y_lo, z], z_send.at[j], z_recv.at[j], z_peer((z + j) % NZ)
        )
        pending.append(arrivals[j])
    near[y_lo, z] = rows_ref[...]
    crossings = [remote(rows_ref, near.at[y_lo, z], y_send.at[0], y_recv.at[0], y_peer)]
    for j in order:
        z_from = (z + NZ - j) % NZ
        arrivals[j].wait_recv()
        crossings.append(
            remote(
                near.at[y_lo, z_from],
                near.at[y_lo, z_from],
                y_send.at[j],
                y_recv.at[j],
                y_peer,
            )
        )
    pending += crossings

    lane = lax.broadcasted_iota(jnp.int32, (2 * N_EXPERTS, half_slots), 0)
    wanted = z * NQ + (
        lax.broadcasted_iota(jnp.int32, (2 * N_EXPERTS, half_slots), 1) // piece
    )
    pick_level, pick_rank = small(lane == wanted), small(lane == wanted + N_EXPERTS)
    row = lax.broadcasted_iota(jnp.int32, (half_rows, half_slots), 0)
    col = lax.broadcasted_iota(jnp.int32, (half_rows, half_slots), 1)
    same_source = (row // TOK) == ((col // CAP) % NZ)
    slot_rank = (col % CAP).astype(jnp.float32)

    slot_flight = {}
    for half in range(2):
        if half == 1:
            for copy in crossings:
                copy.wait_recv()
        y_at = y_lo if half == 0 else 1 - y_lo
        held = (
            near[y_at]
            .astype(jnp.float32)
            .reshape(half_rows, sent + 2 * N_EXPERTS)
            .astype(jnp.bfloat16)
        )
        route = held[:, sent:]
        level, rank = mm(route, pick_level), mm(route, pick_rank)
        chosen = (level > 0.5) & (rank == slot_rank) & same_source
        weigh[half] = jnp.where(chosen, level, 0.0).astype(jnp.bfloat16)
        picked = mm_t(small(chosen), held[:, :sent])
        slots[half] = picked.astype(jnp.bfloat16).reshape(NQ, piece, sent)
        for j in order:
            p = (q + j) % NQ
            slot_flight[half, j] = remote(
                slots.at[half, p],
                inbox.at[0, half, q],
                q_send.at[half, j],
                q_recv.at[half, j],
                q_peer(p),
            )
        inbox[0, half, q] = slots[half, q]
    pending += slot_flight.values()

    mate_flight = []
    for half in range(2):
        for j in (0,) + order:
            q_from = (q + NQ - j) % NQ
            if j:
                slot_flight[half, j].wait_recv()
            mate_flight.append(
                remote(
                    inbox.at[0, half, q_from],
                    inbox.at[1, half, q_from],
                    m_send.at[half, j],
                    m_recv.at[half, j],
                    mate,
                )
            )
    pending += mate_flight

    bin_lane = lax.broadcasted_iota(jnp.int32, (2 * half_slots, 2 * N_EXPERTS), 1)
    bins_at = bin_lane.astype(jnp.float32)

    def run_block(which):
        block = inbox[which].reshape(2 * half_slots, sent)
        x = block[:, :width]
        gate_part, up_part = mm(x, gate_ref[...]), mm(x, up_ref[...])
        activation = gate_part / (1.0 + jnp.exp(-gate_part)) * up_part
        energy = jnp.sum(activation * activation, axis=1, keepdims=True) * (1.0 / HID)
        tail = block[:, width:].astype(jnp.float32)
        high = jnp.sum(jnp.where(bin_lane == me, tail, 0.0), axis=1, keepdims=True)
        low = jnp.sum(
            jnp.where(bin_lane == me + N_EXPERTS, tail, 0.0), axis=1, keepdims=True
        )
        at_high = jnp.where(high == bins_at, energy, 0.0)
        at_low = small(low == bins_at)
        first, second, third = split3(at_high)
        hist = mm_t(first, at_low) + mm_t(second, at_low) + mm_t(third, at_low)
        return activation.astype(jnp.bfloat16), hist

    for load in loads:
        load.wait()
    hidden, hist = run_block(0)
    kept[...] = mm(hidden, down_ref[...])
    for copy in mate_flight:
        copy.wait_recv()
    hidden, more = run_block(1)
    to_mate[...] = (
        mm(hidden, down_ref[...]).astype(jnp.bfloat16).reshape(to_mate.shape)
    )
    mate_out = {}
    for half in (1, 0):
        mate_out[half] = remote(
            to_mate.at[half], from_mate.at[half], o_send.at[half], o_recv.at[half], mate
        )
    pending += mate_out.values()

    hist_out[...] = (hist + more)[: N_CTX * 8].reshape(N_CTX, 8, 2 * N_EXPERTS)
    hist_flight = [
        remote(
            hist_out.at[(ctx + j) % N_CTX],
            hist_in.at[j - 1],
            h_send.at[j - 1],
            h_recv.at[j - 1],
            c_peer(j),
        )
        for j in range(1, N_CTX)
    ]
    pending += hist_flight

    back_flight = {}
    for half in (1, 0):
        mate_out[half].wait_recv()
        total = kept[half * half_slots : (half + 1) * half_slots] + from_mate[
            half
        ].reshape(half_slots, width).astype(jnp.float32)
        back[half] = total.astype(jnp.bfloat16).reshape(NQ, piece, width)
        for j in order:
            p = (q + j) % NQ
            back_flight[half, j] = remote(
                back.at[half, p],
                returned.at[half, q],
                b_send.at[half, j],
                b_recv.at[half, j],
                q_peer(p),
            )
        returned[half, q] = back[half, q]
    pending += back_flight.values()

    def mixed(half):
        for j in order:
            back_flight[half, j].wait_recv()
        return mm(weigh[half], returned[half].reshape(half_slots, width))

    to_y[...] = mixed(1).reshape(NZ, TOK, width).astype(jnp.bfloat16)
    y_flight = [
        remote(to_y.at[j], from_y.at[j], ys_send.at[j], ys_recv.at[j], y_peer)
        for j in range(NZ)
    ]
    pending += y_flight
    own = mixed(0).reshape(NZ, TOK, width)
    for copy in y_flight:
        copy.wait_recv()
    to_z[...] = (own + from_y[...].astype(jnp.float32)).astype(jnp.bfloat16)
    z_flight = []
    for j in order:
        z_to = (z + j) % NZ
        z_flight.append(
            remote(
                to_z.at[z_to],
                from_z.at[j - 1],
                zs_send.at[j - 1],
                zs_recv.at[j - 1],
                z_peer(z_to),
            )
        )
    pending += z_flight
    for copy in hist_flight:
        copy.wait_recv()
    hist = hist_out[ctx]
    for j in range(N_CTX - 1):
        hist = hist + hist_in[j]
    hist_ref[...] = hist
    for copy in z_flight:
        copy.wait_recv()
    total = to_z[z].astype(jnp.float32)
    for j in range(NZ - 1):
        total = total + from_z[j].astype(jnp.float32)
    out_ref[...] = (state_ref[...] + total * scale_ref[:, :1]).astype(jnp.bfloat16)
    for copy in pending:
        copy.wait_send()


def run_experts(rows, state, scale, gate, up, down):
    width = state.shape[1]
    sent = width + 2 * N_EXPERTS
    half_slots, piece = NQ * NZ * CAP, NZ * CAP
    bf16, f32 = jnp.bfloat16, jnp.float32
    dma = pltpu.SemaphoreType.DMA
    vmem = pl.BlockSpec(memory_space=pltpu.VMEM)
    hbm = pl.BlockSpec(memory_space=pl.ANY)
    return pl.pallas_call(
        experts_kernel,
        out_shape=(
            jax.ShapeDtypeStruct((TOK, width), bf16),
            jax.ShapeDtypeStruct((8, 2 * N_EXPERTS), f32),
        ),
        in_specs=[vmem, vmem, vmem, hbm, hbm, hbm],
        out_specs=(vmem, vmem),
        scratch_shapes=[
            pltpu.VMEM(gate.shape, bf16),
            pltpu.VMEM(up.shape, bf16),
            pltpu.VMEM(down.shape, bf16),
            pltpu.VMEM((2, NZ, TOK, rows.shape[1]), bf16),
            pltpu.VMEM((2, NZ * TOK, half_slots), bf16),
            pltpu.VMEM((2, NQ, piece, sent), bf16),
            pltpu.VMEM((2, 2, NQ, piece, sent), bf16),
            pltpu.VMEM((2 * half_slots, width), f32),
            pltpu.VMEM((2, NQ, piece, width), bf16),
            pltpu.VMEM((2, NQ, piece, width), bf16),
            pltpu.VMEM((2, NQ, piece, width), bf16),
            pltpu.VMEM((2, NQ, piece, width), bf16),
            pltpu.VMEM((NZ, TOK, width), bf16),
            pltpu.VMEM((NZ, TOK, width), bf16),
            pltpu.VMEM((NZ, TOK, width), bf16),
            pltpu.VMEM((NZ - 1, TOK, width), bf16),
            pltpu.VMEM((N_CTX, 8, 2 * N_EXPERTS), f32),
            pltpu.VMEM((N_CTX - 1, 8, 2 * N_EXPERTS), f32),
            dma((3,)),
            dma((NZ,)),
            dma((NZ,)),
            dma((NZ,)),
            dma((NZ,)),
            dma((2, NQ)),
            dma((2, NQ)),
            dma((2, NQ)),
            dma((2, NQ)),
            dma((2,)),
            dma((2,)),
            dma((2, NQ)),
            dma((2, NQ)),
            dma((NZ,)),
            dma((NZ,)),
            dma((NZ - 1,)),
            dma((NZ - 1,)),
            dma((N_CTX - 1,)),
            dma((N_CTX - 1,)),
        ],
        compiler_params=pltpu.CompilerParams(
            collective_id=1, has_side_effects=True, vmem_limit_bytes=50 << 20
        ),
        name="experts",
    )(rows, state, scale, gate, up, down)


def route_lanes(expert_ids, gate_levels, bin_ids):
    onehot = expert_ids[:, :, None] == jnp.arange(N_EXPERTS, dtype=jnp.int32)

    def spread(v):
        return jnp.sum(jnp.where(onehot, v[:, :, None], 0), axis=1)

    named = jnp.sum(onehot.astype(jnp.int32), axis=1)
    earlier = jnp.arange(TOK)[:, None] > jnp.arange(TOK)[None, :]
    rank = jnp.sum(jnp.where(earlier[:, :, None], named[None, :, :], 0), axis=1)
    lanes = (spread(bin_ids // 64), spread(bin_ids % 64), spread(gate_levels), rank)
    return jnp.concatenate(lanes, axis=1).astype(jnp.bfloat16)


def key_scores(query_nope, query_rope, lat_rows, rope_rows):
    scores = jnp.einsum("qhl,kl->hqk", query_nope, lat_rows, preferred_element_type=jnp.float32)
    scores = scores + jnp.einsum(
        "qhr,kr->hqk", query_rope, rope_rows, preferred_element_type=jnp.float32
    )
    return scores * softmax_scale


def attend_piece(running, key_piece, query_nope, query_rope, query_pos, query_docs):
    lat_rows, rope_rows, doc_rows = key_piece
    key_pos = jnp.arange(lat_rows.shape[0], dtype=jnp.int32)
    allowed = (key_pos[None, :] <= query_pos[:, None]) & (doc_rows[None, :] == query_docs[:, None])
    scores = jnp.where(
        allowed[None], key_scores(query_nope, query_rope, lat_rows, rope_rows), masked_score
    )
    run_max, run_sum, accum = running
    new_max = jnp.maximum(run_max, jnp.max(scores, axis=2))
    probs = jnp.where(allowed[None], jnp.exp(scores - new_max[:, :, None]), 0.0)
    run_sum = jnp.sum(probs, axis=2)
    accum = jnp.einsum(
        "hqk,kl->hql", probs.astype(jnp.bfloat16), lat_rows, preferred_element_type=jnp.float32
    )
    return (new_max, run_sum, accum)


def project_values(context, uv_weight):
    values = jnp.einsum(
        "hql,hlv->qhv", context, uv_weight, preferred_element_type=jnp.float32
    ).astype(jnp.bfloat16)
    return values.reshape(values.shape[0], values.shape[1] * values.shape[2])


def head_values(running, uv_weight):
    context = (running[2] / running[1][:, :, None]).astype(jnp.bfloat16)
    return project_values(context, uv_weight)


def on_device(
    residual_in,
    norm_gain,
    q_nope,
    q_rope,
    latent,
    k_rope,
    doc_ids,
    uv_weight,
    out_weight,
    expert_ids,
    gate_levels,
    bin_ids,
    gate_weight,
    up_weight,
    down_weight,
):
    block_len, head_count, lat_width = q_nope.shape
    rope_width = k_rope.shape[1]
    query_first = lax.axis_index("ctx") * block_len
    query_pos = query_first + jnp.arange(block_len, dtype=jnp.int32)
    query_rope = q_rope.reshape(block_len, head_count, rope_width)
    keys_local = (latent, k_rope, doc_ids)
    initial = (
        jnp.full((head_count, block_len), masked_score, jnp.float32),
        jnp.zeros((head_count, block_len), jnp.float32),
        jnp.zeros((head_count, block_len, lat_width), jnp.float32),
    )
    running = attend_piece(
        initial,
        (
            lax.all_gather(keys_local[0], "ctx", axis=0, tiled=True),
            lax.all_gather(keys_local[1], "ctx", axis=0, tiled=True),
            lax.all_gather(keys_local[2], "ctx", axis=0, tiled=True),
        ),
        q_nope,
        query_rope,
        query_pos,
        doc_ids,
    )
    attended = project_sum(head_values(running, uv_weight), out_weight)
    stream_state = residual_in.astype(jnp.float32) + attended
    normed = (
        stream_state
        * lax.rsqrt(jnp.mean(stream_state * stream_state, axis=1, keepdims=True) + norm_eps)
        * norm_gain
    ).astype(jnp.bfloat16)
    rows = jnp.concatenate(
        (normed, route_lanes(expert_ids, gate_levels, bin_ids)), axis=1
    )
    scale = 1.0 / jnp.sum(gate_levels.astype(jnp.float32), axis=1, keepdims=True)
    layer_out, hist = run_experts(
        rows,
        stream_state,
        jnp.broadcast_to(scale, (TOK, 128)),
        gate_weight[0],
        up_weight[0],
        down_weight[0],
    )
    histogram = hist[:, : NBINS // 32].reshape(1, NBINS // N_CTX)
    return (layer_out, histogram)


def solution(mesh):
    return jax.shard_map(
        on_device,
        mesh=mesh,
        in_specs=(
            P(("ctx", "exp"), None),
            P(),
            P("ctx", "exp", None),
            P("ctx", "exp"),
            P("ctx", None),
            P("ctx", None),
            P("ctx"),
            P("exp", None, None),
            P("exp", None),
            P(("ctx", "exp"), None),
            P(("ctx", "exp"), None),
            P(("ctx", "exp"), None),
            P("exp", None, "ctx"),
            P("exp", None, "ctx"),
            P("exp", "ctx", None),
        ),
        out_specs=(P(("ctx", "exp"), None), P("exp", "ctx")),
        check_vma=False,
    )
```

time: 650 us -> 224 us (0.34)
  waiting for transfers between devices: 496 us -> 18.9 us
  Pallas kernels: 0 us -> 144 us
  blocking collectives: 44.8 us -> 14.4 us
  starting transfers between devices: 25.4 us -> 0.04 us
  matrix products: 34.9 us -> 13.4 us
  local copies, waits for them, and re-layouts: 21.8 us -> 9.1 us
  other arithmetic: 13.1 us -> 6.26 us
    reduce_scatter x2 -> x0, waiting for transfers between devices: 359 us -> none  [the longest x1 328 us: on_device(): lax.psum_scatter(head_rows(jnp.int32(0), token_count * lax.axis_size('exp...]
    pallas_call x0 -> x2, Pallas kernels: none -> 144 us  [the longest x1 94.2 us: run_experts(): pl.pallas_call(experts_kernel, out_shape=(jax.ShapeDtypeStruct((TOK, widt...]
    all_gather x1 -> x0, waiting for transfers between devices: 91.2 us -> none  [on_device(): lax.all_gather(incoming, 'ctx', axis=1, tiled=True)]
    all_to_all x2 -> x0, starting transfers between devices: 25 us -> none  [the longest x1 12.5 us: on_device(): lax.all_to_all(slot_bins, 'exp', split_axis=0, concat_axis=1, tiled=True)]
    all_to_all x1 -> x0, blocking collectives: 24.6 us -> none  [on_device(): lax.all_to_all(outgoing, 'exp', split_axis=0, concat_axis=1, tiled=True)]
    unnamed x6 -> x1, waiting for transfers between devices: 24.5 us -> 0.68 us
    dot_general x6 -> x0, matrix products: 17.1 us -> none  [the longest x1 4.11 us: head_rows(): return jnp.dot(values, out_weight, preferred_element_type=jnp.float32)]
    unnamed x1 -> x0, other arithmetic: 7.22 us -> none
  transfers between devices with their start and end apart: 7 -> 1, of which waited for: 5 -> 1; matrix products, arithmetic and copies ran while one was open for 4% -> 2% of each run, Pallas kernels for 0% -> 0%
where the time goes in v1:
time: 224 us; the launch traced here: 221 us
  Pallas kernels  144 us (64%)
  waiting for transfers between devices  18.9 us (8%)
  blocking collectives  14.4 us (6%)
  between operations  14.2 us (6%)
  matrix products  13.4 us (6%)
  local copies, waits for them, and re-layouts  9.1 us (4%)
  other arithmetic  6.26 us (3%)
    pallas_call x1, Pallas kernels, run_experts(): pl.pallas_call(experts_kernel, out_shape=(jax.ShapeDtypeStruct((TOK, widt...  94.2 us
    pallas_call x1, Pallas kernels, project_sum(): pl.pallas_call(functools.partial(project_sum_kernel, part_a), out_shape=j...  50 us
    all_gather x1, waiting for transfers between devices, on_device(): lax.all_gather(keys_local[0], 'ctx', axis=0, tiled=True)  18.2 us
    all_gather x1, blocking collectives, on_device(): lax.all_gather(keys_local[2], 'ctx', axis=0, tiled=True)  8.33 us
    unnamed x18, local copies, waits for them, and re-layouts  7.85 us
    dot_general x1, matrix products, project_values(): jnp.einsum('hql,hlv->qhv', context, uv_weight, preferred_element_type=jnp...  7.11 us
    all_gather x1, blocking collectives, on_device(): lax.all_gather(keys_local[1], 'ctx', axis=0, tiled=True)  6.06 us
  transfers between devices with their start and end apart: 1, of which 1 were waited for; matrix products, arithmetic and copies ran while one was open for 2% of the time, Pallas kernels for 0%

profile of v1, /device:TPU:1, one launch (start us, length us, event | category | flops | bytes accessed | tf_op | source)
XLA Modules:
  0.0 220.5 jit_solution(6211096742367026583)
XLA Ops:
  7.2 0.0 copy-start
  7.2 0.0 all-gather.3.cloned.1.call-start
  7.2 0.7 all-gather.3.cloned.1.call-update
  7.9 1.0 copy.28
  8.9 0.7 add_select_fusion.1
  9.6 0.8 convert_reduce_fusion
  10.5 0.1 select_reduce_fusion
  10.6 8.3 %all-gather = s32[4,1,512]{2,1,0:T(1,128)S(1)} all-gather(s32[1,1,512]{2,1,0:T(1,128)} %bitcast.33), channel_id=1, replica_groups=mesh['ctx'=4,'exp'=64] {'ctx'}, dimensions={0}, use_global_device_ids=true | all-gather | bytes 10240 | tf_op jit(solution)/shard_map/all_gather | solution.py:692
  19.0 6.1 %all_gather.11 = bf16[2048,64]{0,1:T(8,128)(2,1)S(1)} all-gather(bf16[512,64]{0,1:T(8,128)(2,1)} %param.20), channel_id=1, replica_groups=mesh['ctx'=4,'exp'=64] {'ctx'}, dimensions={0}, use_global_device_ids=true | all-gather | bytes 327680 | tf_op jit(solution)/shard_map/all_gather | solution.py:691
  25.0 0.8 convert_reduce_fusion.1
  25.8 1.7 fusion.6
  27.5 0.0 copy-start.5
  27.6 18.2 %all-gather.3.cloned.1.call-done = bf16[2048,512]{1,0:T(8,128)(2,1)} async-done(((bf16[512,512]{1,0:T(8,128)(2,1)}), bf16[2048,512]{1,0:T(8,128)(2,1)}) %all-gather.3.cloned.1.call-update) | async-done | bytes 2097168 | tf_op jit(solution)/shard_map/all_gather | solution.py:690
  45.8 0.0 copy-done
  45.8 4.0 %fusion.9 = f32[2048,512,2]{1,0,2:T(8,128)S(1)} fusion(bf16[2048,512]{1,0:T(8,128)(2,1)} %all-gather.3.cloned.1.call-done, bf16[512,2,512]{2,1,0:T(2,128)(2,1)S(1)} %copy-done), kind=kOutput, calls=%fused_computation.11 | convolution fusion | flops 2147483648 | bytes 11534336 | tf_op jit(solution)/shard_map/qhl,kl->hqk/dot_general | solution.py:623
  49.7 2.3 %fusion.26 = (f32[2,512]{1,0:T(2,128)S(1)}, f32[2,512,2048]{1,2,0:T(8,128)S(1)}) fusion(f32[2048,512,2]{1,0,2:T(8,128)S(1)} %fusion.9, bf16[512,2,64]{0,2,1:T(8,128)(2,1)S(1)} %bitcast.31, bf16[2048,64]{0,1:T(8,128)(2,1)S(1)} %all_gather.11, pred[512,2048]{0,1:T(8,128)(4,1)S(1)} %fusion.6), kind=kOutput, calls=%fused_computation.42 | convolution fusion | flops 276823040 | bytes 18223104 | tf_op jit(solution)/shard_map/qhr,kr->hqk/dot_general | solution.py:624
  52.1 0.0 copy-start.4
  52.1 0.0 copy-done.5
  52.1 3.2 %copy-done.4 = f32[2,512,2048]{1,2,0:T(8,128)} copy-done((f32[2,512,2048]{1,2,0:T(8,128)}, f32[2,512,2048]{1,2,0:T(8,128)S(1)}, u32[]{:S(2)}) %copy-start.4) | copy-done | bytes 8388632
  55.3 1.9 fusion
  57.2 0.0 copy-start.1
  57.2 0.0 copy-start.6
  57.2 0.0 copy-start.7
  57.2 7.1 %fusion.11 = bf16[512,2,128]{2,0,1:T(8,128)(2,1)S(1)} fusion(bf16[2,512,128]{2,1,0:T(8,128)(2,1)} %param.22, f32[2,512]{1,0:T(2,128)S(1)} %fusion, f32[2,512,2048]{1,2,0:T(8,128)} %copy-done.4, f32[2,512]{1,0:T(2,128)S(1)} %broadcast_maximum_fusion, pred[512,2048]{0,1:T(8,128)(4,1)} %copy-done.5, bf16[2048,512]{1,0:T(8,128)(2,1)} %all-gather.3.cloned.1.call-done), kind=kOutput, calls=%fused_computation.15 | convolution fusion | flops 2289172480 | bytes 12066816 | tf_op jit(solution)/shard_map/hql,hlv->qhv/dot_general | solution.py:648
  64.3 0.3 copy.30
  64.6 0.2 reshape_reshape.3.values_ref
  64.8 0.0 copy-done.1
  64.8 50.0 %project_sum.1 = f32[8,3584]{1,0:T(8,128)S(1)} custom-call(bf16[8,4,16,256]{3,2,1,0:T(8,128)(2,1)S(1)} %reshape_reshape.3.values_ref, bf16[256,3584]{1,0:T(8,128)(2,1)S(1)} %copy-done.1), custom_call_target="tpu_custom_call" | custom-call | tf_op jit(solution)/shard_map/project_sum/pallas_call | solution.py:220
  114.8 0.0 copy-done.6
  114.8 0.1 multiply_reduce_fusion
  114.9 0.0 copy-done.7
  114.9 0.1 multiply_convert_fusion
  115.0 0.1 concatenate.6.rows_ref
  115.1 0.1 broadcast_in_dim.98.scale_ref
  115.2 0.0 copy-start.2
  115.2 1.5 copy-done.2
  116.7 0.0 copy-start.3
  116.7 1.5 copy-done.3
  118.2 94.2 %experts.1 = (bf16[8,3584]{1,0:T(8,128)(2,1)S(1)}, f32[8,128]{1,0:T(8,128)S(1)}) custom-call(bf16[8,3840]{1,0:T(8,128)(2,1)S(1)} %concatenate.6.rows_ref, f32[8,3584]{1,0:T(8,128)S(1)} %get-tuple-element.11.state_ref, f32[8,128]{1,0:T(8,128)S(1)} %broadcast_in_dim.98.scale_ref, bf16[3584,256]{1,0:T(8,128)(2,1)S(1)} %bitcast.27, ...), custom_call_target="tpu_custom_call" | custom-call | tf_op jit(solution)/shard_map/experts/pallas_call | solution.py:555
  212.4 0.7 reshape.96
  213.0 0.6 copy.35
  (9 shorter events, 0.0 us)
Async XLA Ops:
  7.2 38.6 %copy-start = (bf16[512,2,512]{2,1,0:T(2,128)(2,1)S(1)}, bf16[512,2,512]{2,1,0:T(2,128)(2,1)}, u32[]{:S(2)}) copy-start(bf16[512,2,512]{2,1,0:T(2,128)(2,1)} %param.17) | copy-start | bytes 3145732
  7.2 38.6 %all-gather.3.cloned.1.call-start = ((), (), s32[]{:S(2)}) async-start(), calls=%async_computation | async-start | bytes 2621440 | tf_op jit(solution)/shard_map/all_gather | solution.py:690
  27.5 24.5 %copy-start.5 = (pred[512,2048]{0,1:T(8,128)(4,1)}, pred[512,2048]{0,1:T(8,128)(4,1)S(1)}, u32[]{:S(2)}) copy-start(pred[512,2048]{0,1:T(8,128)(4,1)S(1)} %fusion.6) | copy-start | bytes 3145732
  52.1 3.2 %copy-start.4 = (f32[2,512,2048]{1,2,0:T(8,128)}, f32[2,512,2048]{1,2,0:T(8,128)S(1)}, u32[]{:S(2)}) copy-start(f32[2,512,2048]{1,2,0:T(8,128)S(1)} %get-tuple-element.15) | copy-start | bytes 25165828
  57.2 7.6 %copy-start.1 = (bf16[256,3584]{1,0:T(8,128)(2,1)S(1)}, bf16[256,3584]{1,0:T(8,128)(2,1)}, u32[]{:S(2)}) copy-start(bf16[256,3584]{1,0:T(8,128)(2,1)} %weight_ref.1) | copy-start | bytes 5505028
  57.2 57.6 %copy-start.6 = (bf16[8,3584]{1,0:T(8,128)(2,1)S(1)}, bf16[8,3584]{1,0:T(8,128)(2,1)}, u32[]{:S(2)}) copy-start(bf16[8,3584]{1,0:T(8,128)(2,1)} %param.15) | copy-start | bytes 172036
  57.2 57.7 %copy-start.7 = (f32[3584]{0:T(1024)S(1)}, f32[3584]{0:T(1024)}, u32[]{:S(2)}) copy-start(f32[3584]{0:T(1024)} %param.16) | copy-start | bytes 43012
  115.2 1.5 copy-start.2
  116.7 1.5 copy-start.3
Sparse Core Ops, SparseCore 0:
  9.8 35.8 all-gather.2

commit v2 on v1

--- a/solution.py
+++ b/solution.py
@@ -1,4 +1,5 @@
 import functools
+import math
 
 import jax
 import jax.numpy as jnp
@@ -11,7 +12,7 @@
 NBINS = 2048
 
 
-softmax_scale = 192.0 ** (-0.5)
+exponent_scale = 192.0 ** (-0.5) * math.log2(math.e)
 norm_eps = 1e-06
 masked_score = -1e30
 
@@ -22,6 +23,10 @@
 CAP = 2
 N_CTX = 4
 N_EXPERTS = 64
+ROPE = 64
+VDIM = 128
+KEY_TAIL = 128
+KEY_PIECES = 2
 MESH = pl.DeviceIdType.MESH
 
 
@@ -45,11 +50,42 @@
     pl.semaphore_wait(barrier, len(targets))
 
 
-def project_sum_kernel(
+def small(cond):
+    return cond.astype(jnp.float32).astype(jnp.bfloat16)
+
+
+def split3(v):
+    first = v.astype(jnp.bfloat16)
+    rest = v - first.astype(jnp.float32)
+    second = rest.astype(jnp.bfloat16)
+    third = (rest - second.astype(jnp.float32)).astype(jnp.bfloat16)
+    return first, second, third
+
+
+def mm(a, b):
+    return jnp.dot(a, b, preferred_element_type=jnp.float32)
+
+
+def mm_t(a, b):
+    return lax.dot_general(
+        a, b, (((0,), (0,)), ((), ())), preferred_element_type=jnp.float32
+    )
+
+
+def attend_sum_kernel(
     part_a,
+    query_ref,
+    key_ref,
+    uv_hbm,
+    weight_hbm,
+    out_ref,
+    uv_ref,
+    weight_ref,
+    keys,
+    top,
+    denominator,
+    accum,
     values_ref,
-    weight_ref,
-    out_ref,
     a_first,
     a_slots,
     b_first,
@@ -58,6 +94,8 @@
     a_got,
     b_push,
     b_got,
+    k_send_sem,
+    k_recv_sem,
     a_send_sem,
     a_recv_sem,
     b_send_sem,
@@ -66,7 +104,14 @@
     ap_recv_sem,
     bp_send_sem,
     bp_recv_sem,
+    load_sem,
 ):
+    loads = [
+        pltpu.make_async_copy(uv_hbm, uv_ref, load_sem.at[0]),
+        pltpu.make_async_copy(weight_hbm, weight_ref, load_sem.at[1]),
+    ]
+    for load in loads:
+        load.start()
     width = weight_ref.shape[1]
     half_a, half_b = part_a // 2, (width - part_a) // 2
     me = lax.axis_index("exp")
@@ -80,10 +125,112 @@
     r_peers = [(r + j) % NR for j in range(NR)]
     z_next = [at((z + 1) % NZ, x, y), at((z + NZ - 1) % NZ, x, y)]
     x_next = [at(z, (x + 1) % NX, y), at(z, (x + NX - 1) % NX, y)]
+    ctx = lax.axis_index("ctx")
+    y_lo, core = ctx // 2, ctx % 2
+    mate = {"ctx": y_lo * 2 + 1 - core, "exp": me}
+    across = {"ctx": (1 - y_lo) * 2 + core, "exp": me}
     greet(
         [at(z, p // NY, p % NY) for p in q_peers[1:]]
         + [at(p // NY, x, p % NY) for p in r_peers[1:]]
-    )
+        + [mate, across]
+    )
+
+    piece = key_ref.shape[0] // KEY_PIECES
+
+    def key_copy(back, i, src, target):
+        return pltpu.make_async_remote_copy(
+            src_ref=src,
+            dst_ref=keys.at[back, i],
+            send_sem=k_send_sem.at[back, i],
+            recv_sem=k_recv_sem.at[back, i],
+            device_id=target,
+            device_id_type=MESH,
+        )
+
+    def own_piece(i):
+        return key_ref.at[i * piece : (i + 1) * piece]
+
+    for i in range(KEY_PIECES):
+
+        @pl.when(y_lo == 0)
+        def _():
+            key_copy(1, i, own_piece(i), across).start()
+
+    for i in range(KEY_PIECES):
+
+        @pl.when(core == 0)
+        def _():
+            key_copy(0, i, own_piece(i), mate).start()
+
+    lat = uv_ref.shape[1]
+    doc_lane = key_ref.shape[1] - KEY_TAIL + ROPE
+    query_docs = key_ref[:, doc_lane : doc_lane + 1].astype(jnp.float32)
+    doc_pick = small(lax.broadcasted_iota(jnp.int32, (8, KEY_TAIL), 1) == ROPE)
+
+    def nt(a, b):
+        return lax.dot_general(
+            a, b, (((1,), (1,)), ((), ())), preferred_element_type=jnp.float32
+        )
+
+    def fold(block, first):
+        docs = nt(doc_pick, block[:, lat:])[:1]
+        allowed = query_docs == docs
+        if first:
+            shape = (query_ref.shape[1], block.shape[0])
+            query_at = lax.broadcasted_iota(jnp.int32, shape, 0)
+            key_at = lax.broadcasted_iota(jnp.int32, shape, 1)
+            allowed = allowed & (key_at <= query_at)
+        for head in range(query_ref.shape[0]):
+            scores = jnp.where(allowed, nt(query_ref[head], block), masked_score)
+            peak = jnp.max(scores, axis=1, keepdims=True)
+            if not first:
+                old = top[head][:, :1]
+                peak = jnp.maximum(old, peak)
+                fade = jnp.exp2((old - peak) * exponent_scale)
+            probs = jnp.exp2((scores - peak) * exponent_scale)
+            mass = jnp.sum(probs, axis=1, keepdims=True)
+            mixed = mm(probs.astype(jnp.bfloat16), block[:, :lat])
+            if not first:
+                mass = mass + denominator[head][:, :1] * fade
+                mixed = mixed + accum[head] * fade
+            top[head] = jnp.broadcast_to(peak, top.shape[1:])
+            denominator[head] = jnp.broadcast_to(mass, denominator.shape[1:])
+            accum[head] = mixed
+
+    fold(key_ref[...], True)
+
+    @pl.when(core == 1)
+    def _():
+        for i in range(KEY_PIECES):
+            key_copy(0, i, own_piece(i), mate).wait_recv()
+            fold(keys[0, i], False)
+
+    @pl.when(y_lo == 1)
+    def _():
+        for i in range(KEY_PIECES):
+            key_copy(1, i, own_piece(i), across).wait_recv()
+
+            @pl.when(core == 1)
+            def _():
+                key_copy(0, i, keys.at[1, i], mate).start()
+
+            fold(keys[1, i], False)
+
+    @pl.when(ctx == 2)
+    def _():
+        for i in range(KEY_PIECES):
+            key_copy(0, i, own_piece(i), mate).wait_recv()
+            fold(keys[0, i], False)
+
+    for load in loads:
+        load.wait()
+    for head in range(query_ref.shape[0]):
+        context = (accum[head] / denominator[head][:, :1]).astype(jnp.bfloat16)
+        values_ref[:, :, :, head * VDIM : (head + 1) * VDIM] = (
+            mm(context, uv_ref[head])
+            .astype(jnp.bfloat16)
+            .reshape(NZ, NX, NY * TOK, VDIM)
+        )
 
     def a_own(way, chunk):
         rows = values_ref[chunk].reshape(NX * NY * TOK, values_ref.shape[3])
@@ -209,20 +356,37 @@
     out_ref[:, :part_a] = total
     for copy in [*a_flight.values(), *b_flight.values(), *pushes]:
         copy.wait_send()
-
-
-def project_sum(values, weight, part_a=2048):
-    rows, depth = values.shape
+    for i in range(KEY_PIECES):
+
+        @pl.when(y_lo == 0)
+        def _():
+            key_copy(1, i, own_piece(i), across).wait_send()
+
+        @pl.when((core == 0) | (y_lo == 1))
+        def _():
+            key_copy(0, i, own_piece(i), mate).wait_send()
+
+
+def attend_sum(queries, keys, uv_weight, weight, part_a=2048):
+    heads, rows, depth = queries.shape
     width = weight.shape[1]
     part_b = width - part_a
     bf16 = jnp.bfloat16
     dma = pltpu.SemaphoreType.DMA
     return pl.pallas_call(
-        functools.partial(project_sum_kernel, part_a),
+        functools.partial(attend_sum_kernel, part_a),
         out_shape=jax.ShapeDtypeStruct((TOK, width), jnp.float32),
-        in_specs=[pl.BlockSpec(memory_space=pltpu.VMEM)] * 2,
+        in_specs=[pl.BlockSpec(memory_space=pltpu.VMEM)] * 2
+        + [pl.BlockSpec(memory_space=pltpu.HBM)] * 2,
         out_specs=pl.BlockSpec(memory_space=pltpu.VMEM),
         scratch_shapes=[
+            pltpu.VMEM(uv_weight.shape, bf16),
+            pltpu.VMEM(weight.shape, bf16),
+            pltpu.VMEM((2, KEY_PIECES, rows // KEY_PIECES, depth), bf16),
+            pltpu.VMEM((heads, rows, 128), jnp.float32),
+            pltpu.VMEM((heads, rows, 128), jnp.float32),
+            pltpu.VMEM((heads, rows, uv_weight.shape[1]), jnp.float32),
+            pltpu.VMEM((NZ, NX, NY * TOK, heads * VDIM), bf16),
             pltpu.VMEM((2, NQ * TOK, part_a // 2), bf16),
             pltpu.VMEM((2, NZ - 1, NQ * TOK, part_a // 2), bf16),
             pltpu.VMEM((2, NR * TOK, part_b // 2), bf16),
@@ -231,6 +395,8 @@
             pltpu.VMEM((NQ - 1, TOK, part_a), bf16),
             pltpu.VMEM((NR, TOK, part_b), bf16),
             pltpu.VMEM((NR - 1, TOK, part_b), bf16),
+            dma((2, KEY_PIECES)),
+            dma((2, KEY_PIECES)),
             dma((2, NZ - 1)),
             dma((2, NZ - 1)),
             dma((2, NX - 1)),
@@ -239,34 +405,13 @@
             dma((NQ - 1,)),
             dma((NR - 1,)),
             dma((NR - 1,)),
+            dma((2,)),
         ],
         compiler_params=pltpu.CompilerParams(
-            collective_id=0, has_side_effects=True, vmem_limit_bytes=40 << 20
+            collective_id=0, has_side_effects=True, vmem_limit_bytes=50 << 20
         ),
-        name="project_sum",
-    )(values.reshape(NZ, NX, NY * TOK, depth), weight)
-
-
-def small(cond):
-    return cond.astype(jnp.float32).astype(jnp.bfloat16)
-
-
-def split3(v):
-    first = v.astype(jnp.bfloat16)
-    rest = v - first.astype(jnp.float32)
-    second = rest.astype(jnp.bfloat16)
-    third = (rest - second.astype(jnp.float32)).astype(jnp.bfloat16)
-    return first, second, third
-
-
-def mm(a, b):
-    return jnp.dot(a, b, preferred_element_type=jnp.float32)
-
-
-def mm_t(a, b):
-    return lax.dot_general(
-        a, b, (((0,), (0,)), ((), ())), preferred_element_type=jnp.float32
-    )
+        name="attend_sum",
+    )(queries, keys, uv_weight, weight)
 
 
 def experts_kernel(
@@ -551,7 +696,7 @@
     bf16, f32 = jnp.bfloat16, jnp.float32
     dma = pltpu.SemaphoreType.DMA
     vmem = pl.BlockSpec(memory_space=pltpu.VMEM)
-    hbm = pl.BlockSpec(memory_space=pl.ANY)
+    hbm = pl.BlockSpec(memory_space=pltpu.HBM)
     return pl.pallas_call(
         experts_kernel,
         out_shape=(
@@ -600,7 +745,7 @@
             dma((N_CTX - 1,)),
         ],
         compiler_params=pltpu.CompilerParams(
-            collective_id=1, has_side_effects=True, vmem_limit_bytes=50 << 20
+            collective_id=1, has_side_effects=True, vmem_limit_bytes=60 << 20
         ),
         name="experts",
     )(rows, state, scale, gate, up, down)
@@ -617,43 +762,6 @@
     rank = jnp.sum(jnp.where(earlier[:, :, None], named[None, :, :], 0), axis=1)
     lanes = (spread(bin_ids // 64), spread(bin_ids % 64), spread(gate_levels), rank)
     return jnp.concatenate(lanes, axis=1).astype(jnp.bfloat16)
-
-
-def key_scores(query_nope, query_rope, lat_rows, rope_rows):
-    scores = jnp.einsum("qhl,kl->hqk", query_nope, lat_rows, preferred_element_type=jnp.float32)
-    scores = scores + jnp.einsum(
-        "qhr,kr->hqk", query_rope, rope_rows, preferred_element_type=jnp.float32
-    )
-    return scores * softmax_scale
-
-
-def attend_piece(running, key_piece, query_nope, query_rope, query_pos, query_docs):
-    lat_rows, rope_rows, doc_rows = key_piece
-    key_pos = jnp.arange(lat_rows.shape[0], dtype=jnp.int32)
-    allowed = (key_pos[None, :] <= query_pos[:, None]) & (doc_rows[None, :] == query_docs[:, None])
-    scores = jnp.where(
-        allowed[None], key_scores(query_nope, query_rope, lat_rows, rope_rows), masked_score
-    )
-    run_max, run_sum, accum = running
-    new_max = jnp.maximum(run_max, jnp.max(scores, axis=2))
-    probs = jnp.where(allowed[None], jnp.exp(scores - new_max[:, :, None]), 0.0)
-    run_sum = jnp.sum(probs, axis=2)
-    accum = jnp.einsum(
-        "hqk,kl->hql", probs.astype(jnp.bfloat16), lat_rows, preferred_element_type=jnp.float32
-    )
-    return (new_max, run_sum, accum)
-
-
-def project_values(context, uv_weight):
-    values = jnp.einsum(
-        "hql,hlv->qhv", context, uv_weight, preferred_element_type=jnp.float32
-    ).astype(jnp.bfloat16)
-    return values.reshape(values.shape[0], values.shape[1] * values.shape[2])
-
-
-def head_values(running, uv_weight):
-    context = (running[2] / running[1][:, :, None]).astype(jnp.bfloat16)
-    return project_values(context, uv_weight)
 
 
 def on_device(
@@ -673,30 +781,20 @@
     up_weight,
     down_weight,
 ):
-    block_len, head_count, lat_width = q_nope.shape
-    rope_width = k_rope.shape[1]
-    query_first = lax.axis_index("ctx") * block_len
-    query_pos = query_first + jnp.arange(block_len, dtype=jnp.int32)
-    query_rope = q_rope.reshape(block_len, head_count, rope_width)
-    keys_local = (latent, k_rope, doc_ids)
-    initial = (
-        jnp.full((head_count, block_len), masked_score, jnp.float32),
-        jnp.zeros((head_count, block_len), jnp.float32),
-        jnp.zeros((head_count, block_len, lat_width), jnp.float32),
-    )
-    running = attend_piece(
-        initial,
-        (
-            lax.all_gather(keys_local[0], "ctx", axis=0, tiled=True),
-            lax.all_gather(keys_local[1], "ctx", axis=0, tiled=True),
-            lax.all_gather(keys_local[2], "ctx", axis=0, tiled=True),
-        ),
-        q_nope,
-        query_rope,
-        query_pos,
-        doc_ids,
-    )
-    attended = project_sum(head_values(running, uv_weight), out_weight)
+    block_len, head_count, _ = q_nope.shape
+    spare = jnp.zeros((block_len, KEY_TAIL - ROPE), jnp.bfloat16)
+    queries = jnp.stack(
+        [
+            jnp.concatenate(
+                (q_nope[:, head], q_rope[:, head * ROPE : (head + 1) * ROPE], spare),
+                axis=1,
+            )
+            for head in range(head_count)
+        ]
+    )
+    doc_column = doc_ids[:, None].astype(jnp.bfloat16)
+    keys = jnp.concatenate((latent, k_rope, doc_column, spare[:, 1:]), axis=1)
+    attended = attend_sum(queries, keys, uv_weight, out_weight)
     stream_state = residual_in.astype(jnp.float32) + attended
     normed = (
         stream_state

time: 224 us -> 192 us (0.86)
  Pallas kernels: 144 us -> 178 us
  waiting for transfers between devices: 18.9 us -> 0 us
  blocking collectives: 14.4 us -> 0 us
  matrix products: 13.4 us -> 0 us
  between operations: 14.2 us -> 0.86 us
  other arithmetic: 6.26 us -> 1.21 us
    pallas_call x1, Pallas kernels: 94.2 us -> 115 us  [run_experts(): pl.pallas_call(experts_kernel, out_shape=(jax.ShapeDtypeStruct((TOK, widt...]
    all_gather x1 -> x0, waiting for transfers between devices: 18.2 us -> none  [on_device(): lax.all_gather(keys_local[0], 'ctx', axis=0, tiled=True)]
    all_gather x2 -> x0, blocking collectives: 14.4 us -> none  [the longest x1 8.33 us: on_device(): lax.all_gather(keys_local[2], 'ctx', axis=0, tiled=True)]
    dot_general x3 -> x0, matrix products: 13.4 us -> none  [the longest x1 7.11 us: project_values(): jnp.einsum('hql,hlv->qhv', context, uv_weight, preferred_element_type=jnp...]
    pallas_call x1, Pallas kernels: 50 us -> 62.6 us  [attend_sum(): pl.pallas_call(functools.partial(attend_sum_kernel, part_a), out_shape=ja...]
    unnamed x18 -> x24, local copies, waits for them, and re-layouts: 7.85 us -> 3.17 us
    slice x0 -> x3, local copies, waits for them, and re-layouts: none -> 3.49 us  [the longest x1 3.37 us: on_device(): q_nope[:, head]]
  transfers between devices with their start and end apart: 1 -> 0, of which waited for: 1 -> 0; matrix products, arithmetic and copies ran while one was open for 2% -> 0% of each run, Pallas kernels for 0% -> 0%
where the time goes in v2:
time: 192 us; the launch traced here: 190 us
  Pallas kernels  178 us (93%)
  local copies, waits for them, and re-layouts  9.94 us (5%)
    pallas_call x1, Pallas kernels, run_experts(): pl.pallas_call(experts_kernel, out_shape=(jax.ShapeDtypeStruct((TOK, widt...  115 us
    pallas_call x1, Pallas kernels, attend_sum(): pl.pallas_call(functools.partial(attend_sum_kernel, part_a), out_shape=ja...  62.6 us

profile of v2, /device:TPU:1, one launch (start us, length us, event | category | flops | bytes accessed | tf_op | source)
XLA Modules:
  0.0 189.7 jit_solution(15565421191247357327)
XLA Ops:
  0.6 3.4 %fusion.2 = (bf16[512,1,512]{2,1,0:T(2,128)(2,1)S(1)}, bf16[512,1,512]{2,1,0:T(2,128)(2,1)S(1)}) fusion(bf16[512,2,512]{2,1,0:T(2,128)(2,1)} %param.17), kind=kLoop, calls=%fused_computation.27 | loop fusion | bytes 2097152 | tf_op jit(solution)/shard_map/slice | solution.py:789
  4.0 0.0 copy-start.3
  4.0 0.3 copy_bitcast_fusion
  4.3 0.6 copy-done.3
  4.9 0.1 fusion.3
  5.0 0.1 pad.11.clone
  5.1 0.3 maximum_bitcast_fusion
  5.4 0.0 copy-start.10
  5.4 0.0 copy-start.4
  5.4 0.0 copy-start.2
  5.5 0.1 pad_maximum_fusion.query_ref
  5.6 0.5 copy-done.10
  6.1 0.0 copy-start
  6.1 0.1 convert_element_type.25
  6.2 0.0 copy-done.4
  6.3 0.1 copy.26
  6.4 0.1 pad.3.clone
  6.5 0.0 copy-done.2
  6.5 0.2 maximum_maximum_fusion.key_ref
  6.7 0.4 copy-done
  7.1 0.0 copy-start.5
  7.1 0.0 copy-start.6
  7.1 0.0 copy-start.8
  7.1 0.0 copy-start.7
  7.1 0.0 copy-start.9
  7.1 62.6 %attend_sum.1 = f32[8,3584]{1,0:T(8,128)S(1)} custom-call(bf16[2,512,640]{2,1,0:T(8,128)(2,1)S(1)} %pad_maximum_fusion.query_ref, bf16[512,640]{1,0:T(8,128)(2,1)S(1)} %maximum_maximum_fusion.key_ref, bf16[2,512,128]{2,1,0:T(8,128)(2,1)S(1)} %copy-done, bf16[256,3584]{1,0:T(8,128)(2,1)} %weight_hbm.1), custom_call_target="tpu_custom_call" | custom-call | tf_op jit(solution)/shard_map/attend_sum/pallas_call | solution.py:376
  69.8 0.0 copy-done.5
  69.8 0.1 multiply_reduce_fusion
  69.9 0.0 copy-start.1
  69.9 0.0 copy-done.6
  69.9 0.1 multiply_convert_fusion
  70.0 0.0 copy-done.8
  70.1 0.0 copy-done.7
  70.1 0.0 copy-done.9
  70.1 0.1 convert_reduce_fusion
  70.2 0.1 select_reduce_fusion
  70.3 0.7 concatenate.18.rows_ref
  71.1 0.1 convert_reduce_fusion.1
  71.2 0.7 broadcast_in_dim.70.scale_ref
  71.9 0.0 copy-done.1
  71.9 115.0 %experts.1 = (bf16[8,3584]{1,0:T(8,128)(2,1)}, f32[8,128]{1,0:T(8,128)}) custom-call(bf16[8,3840]{1,0:T(8,128)(2,1)} %concatenate.18.rows_ref, f32[8,3584]{1,0:T(8,128)} %copy-done.1, f32[8,128]{1,0:T(8,128)} %broadcast_in_dim.70.scale_ref, bf16[3584,256]{1,0:T(8,128)(2,1)} %bitcast.12, bf16[3584,256]{1,0:T(8,128)(2,1)} %bitcast.13, bf16[256,3584]{1,0:T(8,128)(2,1)} %bitcast.14), custom_call_target="tpu_custom_call" | custom-call | tf_op jit(solution)/shard_map/experts/pallas_call | solution.py:700
  186.9 1.3 reshape.38
  188.2 1.4 copy.33
  (11 shorter events, 0.1 us)
Async XLA Ops:
  4.0 0.9 copy-start.3
  5.4 0.7 copy-start.10
  5.4 0.8 copy-start.4
  5.4 1.1 copy-start.2
  6.1 1.0 copy-start
  7.1 62.7 %copy-start.5 = (bf16[8,3584]{1,0:T(8,128)(2,1)S(1)}, bf16[8,3584]{1,0:T(8,128)(2,1)}, u32[]{:S(2)}) copy-start(bf16[8,3584]{1,0:T(8,128)(2,1)} %param.15) | copy-start | bytes 172036
  7.1 62.8 %copy-start.6 = (f32[3584]{0:T(1024)S(1)}, f32[3584]{0:T(1024)}, u32[]{:S(2)}) copy-start(f32[3584]{0:T(1024)} %param.16) | copy-start | bytes 43012
  7.1 62.9 %copy-start.8 = (s32[8,8]{1,0:T(8,128)S(1)}, s32[8,8]{1,0:T(8,128)}, u32[]{:S(2)}) copy-start(s32[8,8]{1,0:T(8,128)} %param.26) | copy-start | bytes 772
  7.1 63.0 %copy-start.7 = (s32[8,8]{1,0:T(8,128)S(1)}, s32[8,8]{1,0:T(8,128)}, u32[]{:S(2)}) copy-start(s32[8,8]{1,0:T(8,128)} %param.25) | copy-start | bytes 772
  7.1 63.0 %copy-start.9 = (s32[8,8]{1,0:T(8,128)S(1)}, s32[8,8]{1,0:T(8,128)}, u32[]{:S(2)}) copy-start(s32[8,8]{1,0:T(8,128)} %param.24) | copy-start | bytes 772
  69.9 1.9 %copy-start.1 = (f32[8,3584]{1,0:T(8,128)}, f32[8,3584]{1,0:T(8,128)S(1)}, u32[]{:S(2)}) copy-start(f32[8,3584]{1,0:T(8,128)S(1)} %get-tuple-element.11.state_ref) | copy-start | bytes 344068

commit v3 on v2

--- a/solution.py
+++ b/solution.py
@@ -25,8 +25,9 @@
 N_EXPERTS = 64
 ROPE = 64
 VDIM = 128
-KEY_TAIL = 128
+DOC_ROWS = 16
 KEY_PIECES = 2
+SUBS = 2
 MESH = pl.DeviceIdType.MESH
 
 
@@ -75,13 +76,18 @@
 def attend_sum_kernel(
     part_a,
     query_ref,
-    key_ref,
+    query_rope_ref,
+    latent_ref,
+    rope_ref,
+    doc_ref,
     uv_hbm,
     weight_hbm,
     out_ref,
     uv_ref,
     weight_ref,
+    tail_ref,
     keys,
+    tails,
     top,
     denominator,
     accum,
@@ -96,6 +102,8 @@
     b_got,
     k_send_sem,
     k_recv_sem,
+    t_send_sem,
+    t_recv_sem,
     a_send_sem,
     a_recv_sem,
     b_send_sem,
@@ -113,7 +121,7 @@
     for load in loads:
         load.start()
     width = weight_ref.shape[1]
-    half_a, half_b = part_a // 2, (width - part_a) // 2
+    wide_a, wide_b = part_a // (2 * SUBS), (width - part_a) // (2 * SUBS)
     me = lax.axis_index("exp")
     z, x, y = me // NQ, (me // NY) % NX, me % NY
     q, r = x * NY + y, z * NY + y
@@ -135,53 +143,92 @@
         + [mate, across]
     )
 
-    piece = key_ref.shape[0] // KEY_PIECES
-
-    def key_copy(back, i, src, target):
-        return pltpu.make_async_remote_copy(
-            src_ref=src,
-            dst_ref=keys.at[back, i],
-            send_sem=k_send_sem.at[back, i],
-            recv_sem=k_recv_sem.at[back, i],
-            device_id=target,
-            device_id_type=MESH,
-        )
-
-    def own_piece(i):
-        return key_ref.at[i * piece : (i + 1) * piece]
+    block_len, lat = latent_ref.shape
+    piece = block_len // KEY_PIECES
+    for i in range(KEY_PIECES):
+        tail_ref[i, :ROPE] = rope_ref[:, i * piece : (i + 1) * piece]
+        tail_ref[i, ROPE:] = jnp.broadcast_to(
+            doc_ref[:, i * piece : (i + 1) * piece].astype(jnp.float32),
+            (DOC_ROWS, piece),
+        ).astype(jnp.bfloat16)
+
+    class KeyCopy:
+        def __init__(self, back, i, forward, target):
+            self.copies = [
+                pltpu.make_async_remote_copy(
+                    src_ref=src,
+                    dst_ref=dst.at[back, i],
+                    send_sem=send_sem.at[back, i],
+                    recv_sem=recv_sem.at[back, i],
+                    device_id=target,
+                    device_id_type=MESH,
+                )
+                for src, dst, send_sem, recv_sem in (
+                    (
+                        keys.at[1, i]
+                        if forward
+                        else latent_ref.at[i * piece : (i + 1) * piece],
+                        keys,
+                        k_send_sem,
+                        k_recv_sem,
+                    ),
+                    (
+                        tails.at[1, i] if forward else tail_ref.at[i],
+                        tails,
+                        t_send_sem,
+                        t_recv_sem,
+                    ),
+                )
+            ]
+
+        def start(self):
+            for copy in self.copies:
+                copy.start()
+
+        def wait_recv(self):
+            for copy in self.copies:
+                copy.wait_recv()
+
+        def wait_send(self):
+            for copy in self.copies:
+                copy.wait_send()
 
     for i in range(KEY_PIECES):
 
         @pl.when(y_lo == 0)
         def _():
-            key_copy(1, i, own_piece(i), across).start()
+            KeyCopy(1, i, False, across).start()
 
     for i in range(KEY_PIECES):
 
         @pl.when(core == 0)
         def _():
-            key_copy(0, i, own_piece(i), mate).start()
-
-    lat = uv_ref.shape[1]
-    doc_lane = key_ref.shape[1] - KEY_TAIL + ROPE
-    query_docs = key_ref[:, doc_lane : doc_lane + 1].astype(jnp.float32)
-    doc_pick = small(lax.broadcasted_iota(jnp.int32, (8, KEY_TAIL), 1) == ROPE)
+            KeyCopy(0, i, False, mate).start()
 
     def nt(a, b):
         return lax.dot_general(
             a, b, (((1,), (1,)), ((), ())), preferred_element_type=jnp.float32
         )
 
-    def fold(block, first):
-        docs = nt(doc_pick, block[:, lat:])[:1]
-        allowed = query_docs == docs
-        if first:
-            shape = (query_ref.shape[1], block.shape[0])
+    heads = uv_ref.shape[0]
+    doc_pick = small(lax.broadcasted_iota(jnp.int32, (DOC_ROWS, 128), 0) == 0)
+    query_docs = jnp.concatenate(
+        [mm_t(tail_ref[i, ROPE:], doc_pick)[:, :1] for i in range(KEY_PIECES)], axis=0
+    )
+
+    def fold(block, tail, offset=None):
+        first = offset == 0
+        allowed = query_docs == tail[ROPE : ROPE + 1].astype(jnp.float32)
+        if offset is not None:
+            shape = (block_len, block.shape[0])
             query_at = lax.broadcasted_iota(jnp.int32, shape, 0)
-            key_at = lax.broadcasted_iota(jnp.int32, shape, 1)
+            key_at = lax.broadcasted_iota(jnp.int32, shape, 1) + offset
             allowed = allowed & (key_at <= query_at)
-        for head in range(query_ref.shape[0]):
-            scores = jnp.where(allowed, nt(query_ref[head], block), masked_score)
+        for head in range(heads):
+            nope = query_ref[:, head * lat : (head + 1) * lat]
+            rope = query_rope_ref[:, head * ROPE : (head + 1) * ROPE]
+            raw = nt(nope, block) + mm(rope, tail[:ROPE])
+            scores = jnp.where(allowed, raw, masked_score)
             peak = jnp.max(scores, axis=1, keepdims=True)
             if not first:
                 old = top[head][:, :1]
@@ -189,7 +236,7 @@
                 fade = jnp.exp2((old - peak) * exponent_scale)
             probs = jnp.exp2((scores - peak) * exponent_scale)
             mass = jnp.sum(probs, axis=1, keepdims=True)
-            mixed = mm(probs.astype(jnp.bfloat16), block[:, :lat])
+            mixed = mm(probs.astype(jnp.bfloat16), block)
             if not first:
                 mass = mass + denominator[head][:, :1] * fade
                 mixed = mixed + accum[head] * fade
@@ -197,34 +244,35 @@
             denominator[head] = jnp.broadcast_to(mass, denominator.shape[1:])
             accum[head] = mixed
 
-    fold(key_ref[...], True)
+    for i in range(KEY_PIECES):
+        fold(latent_ref[i * piece : (i + 1) * piece], tail_ref[i], i * piece)
 
     @pl.when(core == 1)
     def _():
         for i in range(KEY_PIECES):
-            key_copy(0, i, own_piece(i), mate).wait_recv()
-            fold(keys[0, i], False)
+            KeyCopy(0, i, False, mate).wait_recv()
+            fold(keys[0, i], tails[0, i])
 
     @pl.when(y_lo == 1)
     def _():
         for i in range(KEY_PIECES):
-            key_copy(1, i, own_piece(i), across).wait_recv()
+            KeyCopy(1, i, False, across).wait_recv()
 
             @pl.when(core == 1)
             def _():
-                key_copy(0, i, keys.at[1, i], mate).start()
-
-            fold(keys[1, i], False)
+                KeyCopy(0, i, True, mate).start()
+
+            fold(keys[1, i], tails[1, i])
 
     @pl.when(ctx == 2)
     def _():
         for i in range(KEY_PIECES):
-            key_copy(0, i, own_piece(i), mate).wait_recv()
-            fold(keys[0, i], False)
+            KeyCopy(0, i, False, mate).wait_recv()
+            fold(keys[0, i], tails[0, i])
 
     for load in loads:
         load.wait()
-    for head in range(query_ref.shape[0]):
+    for head in range(heads):
         context = (accum[head] / denominator[head][:, :1]).astype(jnp.bfloat16)
         values_ref[:, :, :, head * VDIM : (head + 1) * VDIM] = (
             mm(context, uv_ref[head])
@@ -232,74 +280,62 @@
             .reshape(NZ, NX, NY * TOK, VDIM)
         )
 
-    def a_own(way, chunk):
+    def a_own(way, sub, chunk):
         rows = values_ref[chunk].reshape(NX * NY * TOK, values_ref.shape[3])
-        return jnp.dot(
-            rows,
-            weight_ref[:, way * half_a : (way + 1) * half_a],
-            preferred_element_type=jnp.float32,
-        )
-
-    def b_own(way, chunk):
+        start = (way * SUBS + sub) * wide_a
+        return mm(rows, weight_ref[:, start : start + wide_a])
+
+    def b_own(way, sub, chunk):
         rows = values_ref[:, chunk].reshape(NZ * NY * TOK, values_ref.shape[3])
-        return jnp.dot(
-            rows,
-            weight_ref[:, part_a + way * half_b : part_a + (way + 1) * half_b],
-            preferred_element_type=jnp.float32,
-        )
+        start = part_a + (way * SUBS + sub) * wide_b
+        return mm(rows, weight_ref[:, start : start + wide_b])
 
     a_flight, b_flight, pushes = {}, {}, []
 
+    def ring_step(step, here, count, own_of, first, slots, sems, onward, flight):
+        for sub in range(SUBS):
+            for way in range(2):
+                sign = -1 if way == 0 else 1
+                own = own_of(way, sub, (here + sign * (1 + step) + 2 * count) % count)
+                if step == 0:
+                    src = first.at[way, sub]
+                    first[way, sub] = own.astype(jnp.bfloat16)
+                else:
+                    src = slots.at[way, sub, step - 1]
+                    flight[way, sub, step - 1].wait_recv()
+                    slots[way, sub, step - 1] = (
+                        slots[way, sub, step - 1].astype(jnp.float32) + own
+                    ).astype(jnp.bfloat16)
+                flight[way, sub, step] = remote(
+                    src,
+                    slots.at[way, sub, step],
+                    sems[0].at[way, sub, step],
+                    sems[1].at[way, sub, step],
+                    onward[way],
+                )
+
     def a_step(step):
-        for way in range(2):
-            sign = -1 if way == 0 else 1
-            own = a_own(way, (z + sign * (1 + step) + 2 * NZ) % NZ)
-            if step == 0:
-                src = a_first.at[way]
-                a_first[way] = own.astype(jnp.bfloat16)
-            else:
-                src = a_slots.at[way, step - 1]
-                a_flight[way, step - 1].wait_recv()
-                a_slots[way, step - 1] = (
-                    a_slots[way, step - 1].astype(jnp.float32) + own
+        ring_step(
+            step, z, NZ, a_own, a_first, a_slots,
+            (a_send_sem, a_recv_sem), z_next, a_flight,
+        )
+
+    def b_step(step):
+        ring_step(
+            step, x, NX, b_own, b_first, b_slots,
+            (b_send_sem, b_recv_sem), x_next, b_flight,
+        )
+
+    def a_push_out():
+        for sub in range(SUBS):
+            for way in range(2):
+                own = a_own(way, sub, z)
+                a_flight[way, sub, NZ - 2].wait_recv()
+                own = own + a_slots[way, sub, NZ - 2].astype(jnp.float32)
+                start = (way * SUBS + sub) * wide_a
+                a_push[:, :, start : start + wide_a] = own.reshape(
+                    NQ, TOK, wide_a
                 ).astype(jnp.bfloat16)
-            a_flight[way, step] = remote(
-                src,
-                a_slots.at[way, step],
-                a_send_sem.at[way, step],
-                a_recv_sem.at[way, step],
-                z_next[way],
-            )
-
-    def b_step(step):
-        for way in range(2):
-            sign = -1 if way == 0 else 1
-            own = b_own(way, (x + sign * (1 + step) + 2 * NX) % NX)
-            if step == 0:
-                src = b_first.at[way]
-                b_first[way] = own.astype(jnp.bfloat16)
-            else:
-                src = b_slots.at[way, step - 1]
-                b_flight[way, step - 1].wait_recv()
-                b_slots[way, step - 1] = (
-                    b_slots[way, step - 1].astype(jnp.float32) + own
-                ).astype(jnp.bfloat16)
-            b_flight[way, step] = remote(
-                src,
-                b_slots.at[way, step],
-                b_send_sem.at[way, step],
-                b_recv_sem.at[way, step],
-                x_next[way],
-            )
-
-    def a_push_out():
-        for way in range(2):
-            own = a_own(way, z)
-            a_flight[way, NZ - 2].wait_recv()
-            own = own + a_slots[way, NZ - 2].astype(jnp.float32)
-            a_push[:, :, way * half_a : (way + 1) * half_a] = own.reshape(
-                NQ, TOK, half_a
-            ).astype(jnp.bfloat16)
         for j in range(1, NQ):
             p = q_peers[j]
             pushes.append(
@@ -313,13 +349,15 @@
             )
 
     def b_push_out():
-        for way in range(2):
-            own = b_own(way, x)
-            b_flight[way, NX - 2].wait_recv()
-            own = own + b_slots[way, NX - 2].astype(jnp.float32)
-            b_push[:, :, way * half_b : (way + 1) * half_b] = own.reshape(
-                NR, TOK, half_b
-            ).astype(jnp.bfloat16)
+        for sub in range(SUBS):
+            for way in range(2):
+                own = b_own(way, sub, x)
+                b_flight[way, sub, NX - 2].wait_recv()
+                own = own + b_slots[way, sub, NX - 2].astype(jnp.float32)
+                start = (way * SUBS + sub) * wide_b
+                b_push[:, :, start : start + wide_b] = own.reshape(
+                    NR, TOK, wide_b
+                ).astype(jnp.bfloat16)
         for j in range(1, NR):
             p = r_peers[j]
             pushes.append(
@@ -360,47 +398,53 @@
 
         @pl.when(y_lo == 0)
         def _():
-            key_copy(1, i, own_piece(i), across).wait_send()
+            KeyCopy(1, i, False, across).wait_send()
 
         @pl.when((core == 0) | (y_lo == 1))
         def _():
-            key_copy(0, i, own_piece(i), mate).wait_send()
-
-
-def attend_sum(queries, keys, uv_weight, weight, part_a=2048):
-    heads, rows, depth = queries.shape
+            KeyCopy(0, i, False, mate).wait_send()
+
+
+def attend_sum(q_nope, q_rope, latent, rope_t, docs, uv_weight, weight, part_a=2048):
+    heads, lat = uv_weight.shape[:2]
+    rows = latent.shape[0]
     width = weight.shape[1]
     part_b = width - part_a
+    wide_a, wide_b = part_a // (2 * SUBS), part_b // (2 * SUBS)
     bf16 = jnp.bfloat16
     dma = pltpu.SemaphoreType.DMA
     return pl.pallas_call(
         functools.partial(attend_sum_kernel, part_a),
         out_shape=jax.ShapeDtypeStruct((TOK, width), jnp.float32),
-        in_specs=[pl.BlockSpec(memory_space=pltpu.VMEM)] * 2
+        in_specs=[pl.BlockSpec(memory_space=pltpu.VMEM)] * 5
         + [pl.BlockSpec(memory_space=pltpu.HBM)] * 2,
         out_specs=pl.BlockSpec(memory_space=pltpu.VMEM),
         scratch_shapes=[
             pltpu.VMEM(uv_weight.shape, bf16),
             pltpu.VMEM(weight.shape, bf16),
-            pltpu.VMEM((2, KEY_PIECES, rows // KEY_PIECES, depth), bf16),
+            pltpu.VMEM((KEY_PIECES, ROPE + DOC_ROWS, rows // KEY_PIECES), bf16),
+            pltpu.VMEM((2, KEY_PIECES, rows // KEY_PIECES, lat), bf16),
+            pltpu.VMEM((2, KEY_PIECES, ROPE + DOC_ROWS, rows // KEY_PIECES), bf16),
             pltpu.VMEM((heads, rows, 128), jnp.float32),
             pltpu.VMEM((heads, rows, 128), jnp.float32),
-            pltpu.VMEM((heads, rows, uv_weight.shape[1]), jnp.float32),
+            pltpu.VMEM((heads, rows, lat), jnp.float32),
             pltpu.VMEM((NZ, NX, NY * TOK, heads * VDIM), bf16),
-            pltpu.VMEM((2, NQ * TOK, part_a // 2), bf16),
-            pltpu.VMEM((2, NZ - 1, NQ * TOK, part_a // 2), bf16),
-            pltpu.VMEM((2, NR * TOK, part_b // 2), bf16),
-            pltpu.VMEM((2, NX - 1, NR * TOK, part_b // 2), bf16),
+            pltpu.VMEM((2, SUBS, NQ * TOK, wide_a), bf16),
+            pltpu.VMEM((2, SUBS, NZ - 1, NQ * TOK, wide_a), bf16),
+            pltpu.VMEM((2, SUBS, NR * TOK, wide_b), bf16),
+            pltpu.VMEM((2, SUBS, NX - 1, NR * TOK, wide_b), bf16),
             pltpu.VMEM((NQ, TOK, part_a), bf16),
             pltpu.VMEM((NQ - 1, TOK, part_a), bf16),
             pltpu.VMEM((NR, TOK, part_b), bf16),
             pltpu.VMEM((NR - 1, TOK, part_b), bf16),
             dma((2, KEY_PIECES)),
             dma((2, KEY_PIECES)),
-            dma((2, NZ - 1)),
-            dma((2, NZ - 1)),
-            dma((2, NX - 1)),
-            dma((2, NX - 1)),
+            dma((2, KEY_PIECES)),
+            dma((2, KEY_PIECES)),
+            dma((2, SUBS, NZ - 1)),
+            dma((2, SUBS, NZ - 1)),
+            dma((2, SUBS, NX - 1)),
+            dma((2, SUBS, NX - 1)),
             dma((NQ - 1,)),
             dma((NQ - 1,)),
             dma((NR - 1,)),
@@ -408,10 +452,10 @@
             dma((2,)),
         ],
         compiler_params=pltpu.CompilerParams(
-            collective_id=0, has_side_effects=True, vmem_limit_bytes=50 << 20
+            collective_id=0, has_side_effects=True, vmem_limit_bytes=60 << 20
         ),
         name="attend_sum",
-    )(queries, keys, uv_weight, weight)
+    )(q_nope, q_rope, latent, rope_t, docs, uv_weight, weight)
 
 
 def experts_kernel(
@@ -782,19 +826,15 @@
     down_weight,
 ):
     block_len, head_count, _ = q_nope.shape
-    spare = jnp.zeros((block_len, KEY_TAIL - ROPE), jnp.bfloat16)
-    queries = jnp.stack(
-        [
-            jnp.concatenate(
-                (q_nope[:, head], q_rope[:, head * ROPE : (head + 1) * ROPE], spare),
-                axis=1,
-            )
-            for head in range(head_count)
-        ]
-    )
-    doc_column = doc_ids[:, None].astype(jnp.bfloat16)
-    keys = jnp.concatenate((latent, k_rope, doc_column, spare[:, 1:]), axis=1)
-    attended = attend_sum(queries, keys, uv_weight, out_weight)
+    attended = attend_sum(
+        q_nope.reshape(block_len, head_count * q_nope.shape[2]),
+        q_rope,
+        latent,
+        k_rope.T,
+        doc_ids.reshape(1, block_len),
+        uv_weight,
+        out_weight,
+    )
     stream_state = residual_in.astype(jnp.float32) + attended
     normed = (
         stream_state

time: 192 us -> 187 us (0.974)
  local copies, waits for them, and re-layouts: 9.94 us -> 6.65 us
    slice x3 -> x0, local copies, waits for them, and re-layouts: 3.49 us -> none  [the longest x1 3.37 us: on_device(): q_nope[:, head]]
    unnamed x24 -> x14, local copies, waits for them, and re-layouts: 3.17 us -> 3.93 us
where the time goes in v3:
time: 187 us; the launch traced here: 186 us
  Pallas kernels  177 us (95%)
  local copies, waits for them, and re-layouts  6.65 us (4%)
    pallas_call x1, Pallas kernels, run_experts(): pl.pallas_call(experts_kernel, out_shape=(jax.ShapeDtypeStruct((TOK, widt...  114 us
    pallas_call x1, Pallas kernels, attend_sum(): pl.pallas_call(functools.partial(attend_sum_kernel, part_a), out_shape=ja...  63.5 us
    unnamed x14, local copies, waits for them, and re-layouts  3.93 us

profile of v3, /device:TPU:1, one launch (start us, length us, event | category | flops | bytes accessed | tf_op | source)
XLA Modules:
  0.0 186.0 jit_solution(13526272267117843962)
XLA Ops:
  0.6 2.5 %copy.17 = bf16[64,8,2,512]{3,1,2,0:T(8,128)(2,1)} copy(bf16[64,8,2,512]{3,2,1,0:T(2,128)(2,1)} %bitcast.12) | data formatting | bytes 2097152
  3.1 0.0 copy-start.1
  3.1 0.0 copy-start.2
  3.1 0.0 copy-start.4
  3.1 0.0 copy-start.3
  3.1 0.0 copy-start.5
  3.1 63.5 %attend_sum.1 = f32[8,3584]{1,0:T(8,128)} custom-call(bf16[512,1024]{1,0:T(8,128)(2,1)} %bitcast.8, bf16[512,128]{1,0:T(8,128)(2,1)} %query_rope_ref.1, bf16[512,512]{1,0:T(8,128)(2,1)} %latent_ref.1, bf16[64,512]{1,0:T(8,128)(2,1)} %bitcast.13, s32[1,512]{1,0:T(1,128)} %bitcast.15, bf16[2,512,128]{2,1,0:T(8,128)(2,1)} %uv_hbm.1, bf16[256,3584]{1,0:T(8,128)(2,1)} %weight_hbm.1), custom_call_target="tpu_custom_call" | custom-call | tf_op jit(solution)/shard_map/attend_sum/pallas_call | solution.py:416
  66.6 0.0 copy-done.1
  66.6 1.0 multiply_reduce_fusion
  67.7 0.0 copy-start
  67.7 0.0 copy-done.2
  67.7 0.1 multiply_convert_fusion
  67.8 0.0 copy-done.4
  67.8 0.0 copy-done.3
  67.8 0.0 copy-done.5
  67.8 0.1 convert_reduce_fusion
  68.0 0.1 select_reduce_fusion
  68.1 0.7 concatenate.6.rows_ref
  68.8 0.1 convert_reduce_fusion.1
  68.9 0.7 broadcast_in_dim.65.scale_ref
  69.6 0.0 copy-done
  69.6 113.6 %experts.1 = (bf16[8,3584]{1,0:T(8,128)(2,1)}, f32[8,128]{1,0:T(8,128)}) custom-call(bf16[8,3840]{1,0:T(8,128)(2,1)} %concatenate.6.rows_ref, f32[8,3584]{1,0:T(8,128)} %copy-done, f32[8,128]{1,0:T(8,128)} %broadcast_in_dim.65.scale_ref, bf16[3584,256]{1,0:T(8,128)(2,1)} %bitcast.9, bf16[3584,256]{1,0:T(8,128)(2,1)} %bitcast.10, bf16[256,3584]{1,0:T(8,128)(2,1)} %bitcast.11), custom_call_target="tpu_custom_call" | custom-call | tf_op jit(solution)/shard_map/experts/pallas_call | solution.py:744
  183.2 1.3 reshape.45
  184.6 1.4 copy.19
  (8 shorter events, 0.0 us)
Async XLA Ops:
  3.1 63.5 %copy-start.1 = (bf16[8,3584]{1,0:T(8,128)(2,1)S(1)}, bf16[8,3584]{1,0:T(8,128)(2,1)}, u32[]{:S(2)}) copy-start(bf16[8,3584]{1,0:T(8,128)(2,1)} %param.15) | copy-start | bytes 172036
  3.1 64.6 %copy-start.2 = (f32[3584]{0:T(1024)S(1)}, f32[3584]{0:T(1024)}, u32[]{:S(2)}) copy-start(f32[3584]{0:T(1024)} %param.16) | copy-start | bytes 43012
  3.1 64.7 %copy-start.4 = (s32[8,8]{1,0:T(8,128)S(1)}, s32[8,8]{1,0:T(8,128)}, u32[]{:S(2)}) copy-start(s32[8,8]{1,0:T(8,128)} %param.26) | copy-start | bytes 772
  3.1 64.7 %copy-start.3 = (s32[8,8]{1,0:T(8,128)S(1)}, s32[8,8]{1,0:T(8,128)}, u32[]{:S(2)}) copy-start(s32[8,8]{1,0:T(8,128)} %param.25) | copy-start | bytes 772
  3.1 64.7 %copy-start.5 = (s32[8,8]{1,0:T(8,128)S(1)}, s32[8,8]{1,0:T(8,128)}, u32[]{:S(2)}) copy-start(s32[8,8]{1,0:T(8,128)} %param.24) | copy-start | bytes 772
  67.7 1.9 %copy-start = (f32[8,3584]{1,0:T(8,128)}, f32[8,3584]{1,0:T(8,128)S(1)}, u32[]{:S(2)}) copy-start(f32[8,3584]{1,0:T(8,128)S(1)} %get-tuple-element.11.state_ref) | copy-start | bytes 344068

commit v4 on v3

--- a/solution.py
+++ b/solution.py
@@ -247,28 +247,37 @@
     for i in range(KEY_PIECES):
         fold(latent_ref[i * piece : (i + 1) * piece], tail_ref[i], i * piece)
 
-    @pl.when(core == 1)
-    def _():
-        for i in range(KEY_PIECES):
-            KeyCopy(0, i, False, mate).wait_recv()
-            fold(keys[0, i], tails[0, i])
-
-    @pl.when(y_lo == 1)
-    def _():
-        for i in range(KEY_PIECES):
-            KeyCopy(1, i, False, across).wait_recv()
+    def fold_from(back, i, target):
+        KeyCopy(back, i, False, target).wait_recv()
+        if back == 1:
 
             @pl.when(core == 1)
             def _():
                 KeyCopy(0, i, True, mate).start()
 
-            fold(keys[1, i], tails[1, i])
-
-    @pl.when(ctx == 2)
+        fold(keys[back, i], tails[back, i])
+
+    @pl.when(ctx == 1)
     def _():
         for i in range(KEY_PIECES):
-            KeyCopy(0, i, False, mate).wait_recv()
-            fold(keys[0, i], tails[0, i])
+            fold_from(0, i, mate)
+
+    for i in range(KEY_PIECES):
+
+        @pl.when(y_lo == 1)
+        def _():
+            fold_from(1, i, across)
+
+        if i == 0:
+
+            @pl.when(ctx == 3)
+            def _():
+                for k in range(KEY_PIECES):
+                    fold_from(0, k, mate)
+
+        @pl.when(ctx == 2)
+        def _():
+            fold_from(0, i, mate)
 
     for load in loads:
         load.wait()
@@ -481,6 +490,7 @@
     returned,
     to_y,
     from_y,
+    own,
     to_z,
     from_z,
     hist_out,
@@ -540,27 +550,44 @@
     )
     pending = []
 
-    order = (1, 7, 2, 6, 3, 5, 4)
-    arrivals = {}
-    for j in order:
-        arrivals[j] = remote(
-            rows_ref, near.at[y_lo, z], z_send.at[j], z_recv.at[j], z_peer((z + j) % NZ)
-        )
-        pending.append(arrivals[j])
+    order = (4, 3, 5, 2, 6, 1, 7)
     near[y_lo, z] = rows_ref[...]
-    crossings = [remote(rows_ref, near.at[y_lo, z], y_send.at[0], y_recv.at[0], y_peer)]
-    for j in order:
-        z_from = (z + NZ - j) % NZ
-        arrivals[j].wait_recv()
-        crossings.append(
-            remote(
-                near.at[y_lo, z_from],
-                near.at[y_lo, z_from],
-                y_send.at[j],
-                y_recv.at[j],
-                y_peer,
-            )
-        )
+    hops = NZ // 2
+    middle = rows_ref.shape[1] // 2
+    onward = (z_peer((z + 1) % NZ), z_peer((z + NZ - 1) % NZ))
+    ring = {}
+
+    def pass_on(way, step, src, dst):
+        ring[way, step] = remote(
+            src, dst, z_send.at[way, step], z_recv.at[way, step], onward[way]
+        )
+        pending.append(ring[way, step])
+
+    crossings = []
+
+    def cross(src, dst):
+        n = len(crossings)
+        crossings.append(remote(src, dst, y_send.at[n], y_recv.at[n], y_peer))
+
+    for way in range(2):
+        pass_on(way, 0, rows_ref, near.at[y_lo, z])
+    cross(rows_ref, near.at[y_lo, z])
+    for step in range(1, hops):
+        for way in range(2):
+            z_from = (z + (NZ - step if way == 0 else step)) % NZ
+            ring[way, step - 1].wait_recv()
+            held = near.at[y_lo, z_from]
+            if step < hops - 1:
+                pass_on(way, step, held, held)
+            else:
+                side = pl.ds(way * middle, middle)
+                part = near.at[y_lo, z_from, :, side]
+                pass_on(way, step, part, part)
+            cross(held, held)
+    for way in range(2):
+        ring[way, hops - 1].wait_recv()
+    held = near.at[y_lo, (z + hops) % NZ]
+    cross(held, held)
     pending += crossings
 
     lane = lax.broadcasted_iota(jnp.int32, (2 * N_EXPERTS, half_slots), 0)
@@ -573,6 +600,7 @@
     same_source = (row // TOK) == ((col // CAP) % NZ)
     slot_rank = (col % CAP).astype(jnp.float32)
 
+    q_order = (1, 2, 3, 4, 5, 6, 7)
     slot_flight = {}
     for half in range(2):
         if half == 1:
@@ -591,7 +619,7 @@
         weigh[half] = jnp.where(chosen, level, 0.0).astype(jnp.bfloat16)
         picked = mm_t(small(chosen), held[:, :sent])
         slots[half] = picked.astype(jnp.bfloat16).reshape(NQ, piece, sent)
-        for j in order:
+        for j in q_order:
             p = (q + j) % NQ
             slot_flight[half, j] = remote(
                 slots.at[half, p],
@@ -605,7 +633,7 @@
 
     mate_flight = []
     for half in range(2):
-        for j in (0,) + order:
+        for j in (0,) + q_order:
             q_from = (q + NQ - j) % NQ
             if j:
                 slot_flight[half, j].wait_recv()
@@ -677,7 +705,7 @@
             half
         ].reshape(half_slots, width).astype(jnp.float32)
         back[half] = total.astype(jnp.bfloat16).reshape(NQ, piece, width)
-        for j in order:
+        for j in q_order:
             p = (q + j) % NQ
             back_flight[half, j] = remote(
                 back.at[half, p],
@@ -690,32 +718,34 @@
     pending += back_flight.values()
 
     def mixed(half):
-        for j in order:
+        for j in q_order:
             back_flight[half, j].wait_recv()
         return mm(weigh[half], returned[half].reshape(half_slots, width))
 
     to_y[...] = mixed(1).reshape(NZ, TOK, width).astype(jnp.bfloat16)
-    y_flight = [
-        remote(to_y.at[j], from_y.at[j], ys_send.at[j], ys_recv.at[j], y_peer)
-        for j in range(NZ)
-    ]
-    pending += y_flight
-    own = mixed(0).reshape(NZ, TOK, width)
-    for copy in y_flight:
-        copy.wait_recv()
-    to_z[...] = (own + from_y[...].astype(jnp.float32)).astype(jnp.bfloat16)
+    y_flight = {}
+    for j in order + (0,):
+        z_to = (z + j) % NZ
+        y_flight[j] = remote(
+            to_y.at[z_to], from_y.at[z_to], ys_send.at[j], ys_recv.at[j], y_peer
+        )
+    pending += y_flight.values()
+    own[...] = mixed(0).reshape(NZ, TOK, width)
     z_flight = []
-    for j in order:
+    for j in order + (0,):
         z_to = (z + j) % NZ
-        z_flight.append(
-            remote(
-                to_z.at[z_to],
-                from_z.at[j - 1],
-                zs_send.at[j - 1],
-                zs_recv.at[j - 1],
-                z_peer(z_to),
+        y_flight[j].wait_recv()
+        to_z[z_to] = (own[z_to] + from_y[z_to].astype(jnp.float32)).astype(jnp.bfloat16)
+        if j:
+            z_flight.append(
+                remote(
+                    to_z.at[z_to],
+                    from_z.at[j - 1],
+                    zs_send.at[j - 1],
+                    zs_recv.at[j - 1],
+                    z_peer(z_to),
+                )
             )
-        )
     pending += z_flight
     for copy in hist_flight:
         copy.wait_recv()
@@ -764,13 +794,14 @@
             pltpu.VMEM((2, NQ, piece, width), bf16),
             pltpu.VMEM((NZ, TOK, width), bf16),
             pltpu.VMEM((NZ, TOK, width), bf16),
+            pltpu.VMEM((NZ, TOK, width), f32),
             pltpu.VMEM((NZ, TOK, width), bf16),
             pltpu.VMEM((NZ - 1, TOK, width), bf16),
             pltpu.VMEM((N_CTX, 8, 2 * N_EXPERTS), f32),
             pltpu.VMEM((N_CTX - 1, 8, 2 * N_EXPERTS), f32),
             dma((3,)),
-            dma((NZ,)),
-            dma((NZ,)),
+            dma((2, NZ // 2)),
+            dma((2, NZ // 2)),
             dma((NZ,)),
             dma((NZ,)),
             dma((2, NQ)),

time: 187 us -> 177 us (0.947)
  Pallas kernels: 177 us -> 168 us
    pallas_call x1, Pallas kernels: 114 us -> 105 us  [run_experts(): pl.pallas_call(experts_kernel, out_shape=(jax.ShapeDtypeStruct((TOK, widt...]
where the time goes in v4:
time: 177 us
  Pallas kernels  168 us (95%)
  local copies, waits for them, and re-layouts  6.65 us (4%)
    pallas_call x1, Pallas kernels, run_experts(): pl.pallas_call(experts_kernel, out_shape=(jax.ShapeDtypeStruct((TOK, widt...  105 us
    pallas_call x1, Pallas kernels, attend_sum(): pl.pallas_call(functools.partial(attend_sum_kernel, part_a), out_shape=ja...  63.5 us
    unnamed x14, local copies, waits for them, and re-layouts  3.93 us

profile of v4, /device:TPU:1, one launch (start us, length us, event | category | flops | bytes accessed | tf_op | source)
XLA Modules:
  0.0 177.2 jit_solution(9834617853450960862)
XLA Ops:
  0.6 2.5 %copy.17 = bf16[64,8,2,512]{3,1,2,0:T(8,128)(2,1)} copy(bf16[64,8,2,512]{3,2,1,0:T(2,128)(2,1)} %bitcast.12) | data formatting | bytes 2097152
  3.1 0.0 copy-start.1
  3.1 0.0 copy-start.2
  3.1 0.0 copy-start.4
  3.1 0.0 copy-start.3
  3.1 0.0 copy-start.5
  3.1 63.5 %attend_sum.1 = f32[8,3584]{1,0:T(8,128)} custom-call(bf16[512,1024]{1,0:T(8,128)(2,1)} %bitcast.8, bf16[512,128]{1,0:T(8,128)(2,1)} %query_rope_ref.1, bf16[512,512]{1,0:T(8,128)(2,1)} %latent_ref.1, bf16[64,512]{1,0:T(8,128)(2,1)} %bitcast.13, s32[1,512]{1,0:T(1,128)} %bitcast.15, bf16[2,512,128]{2,1,0:T(8,128)(2,1)} %uv_hbm.1, bf16[256,3584]{1,0:T(8,128)(2,1)} %weight_hbm.1), custom_call_target="tpu_custom_call" | custom-call | tf_op jit(solution)/shard_map/attend_sum/pallas_call | solution.py:425
  66.7 0.0 copy-done.1
  66.7 1.0 multiply_reduce_fusion
  67.7 0.0 copy-start
  67.7 0.0 copy-done.2
  67.7 0.1 multiply_convert_fusion
  67.8 0.0 copy-done.4
  67.8 0.0 copy-done.3
  67.9 0.0 copy-done.5
  67.9 0.1 convert_reduce_fusion
  68.0 0.1 select_reduce_fusion
  68.1 0.7 concatenate.6.rows_ref
  68.9 0.1 convert_reduce_fusion.1
  69.0 0.7 broadcast_in_dim.65.scale_ref
  69.6 0.0 copy-done
  69.6 104.7 %experts.1 = (bf16[8,3584]{1,0:T(8,128)(2,1)}, f32[8,128]{1,0:T(8,128)}) custom-call(bf16[8,3840]{1,0:T(8,128)(2,1)} %concatenate.6.rows_ref, f32[8,3584]{1,0:T(8,128)} %copy-done, f32[8,128]{1,0:T(8,128)} %broadcast_in_dim.65.scale_ref, bf16[3584,256]{1,0:T(8,128)(2,1)} %bitcast.9, bf16[3584,256]{1,0:T(8,128)(2,1)} %bitcast.10, bf16[256,3584]{1,0:T(8,128)(2,1)} %bitcast.11), custom_call_target="tpu_custom_call" | custom-call | tf_op jit(solution)/shard_map/experts/pallas_call | solution.py:774
  174.4 1.3 reshape.45
  175.7 1.4 copy.19
  (8 shorter events, 0.0 us)
Async XLA Ops:
  3.1 63.6 %copy-start.1 = (bf16[8,3584]{1,0:T(8,128)(2,1)S(1)}, bf16[8,3584]{1,0:T(8,128)(2,1)}, u32[]{:S(2)}) copy-start(bf16[8,3584]{1,0:T(8,128)(2,1)} %param.15) | copy-start | bytes 172036
  3.1 64.6 %copy-start.2 = (f32[3584]{0:T(1024)S(1)}, f32[3584]{0:T(1024)}, u32[]{:S(2)}) copy-start(f32[3584]{0:T(1024)} %param.16) | copy-start | bytes 43012
  3.1 64.7 %copy-start.4 = (s32[8,8]{1,0:T(8,128)S(1)}, s32[8,8]{1,0:T(8,128)}, u32[]{:S(2)}) copy-start(s32[8,8]{1,0:T(8,128)} %param.26) | copy-start | bytes 772
  3.1 64.7 %copy-start.3 = (s32[8,8]{1,0:T(8,128)S(1)}, s32[8,8]{1,0:T(8,128)}, u32[]{:S(2)}) copy-start(s32[8,8]{1,0:T(8,128)} %param.25) | copy-start | bytes 772
  3.1 64.8 %copy-start.5 = (s32[8,8]{1,0:T(8,128)S(1)}, s32[8,8]{1,0:T(8,128)}, u32[]{:S(2)}) copy-start(s32[8,8]{1,0:T(8,128)} %param.24) | copy-start | bytes 772
  67.7 1.9 %copy-start = (f32[8,3584]{1,0:T(8,128)}, f32[8,3584]{1,0:T(8,128)S(1)}, u32[]{:S(2)}) copy-start(f32[8,3584]{1,0:T(8,128)S(1)} %get-tuple-element.11.state_ref) | copy-start | bytes 344068

commit v5 on v4

--- a/solution.py
+++ b/solution.py
@@ -98,6 +98,8 @@
     b_slots,
     a_push,
     a_got,
+    b_mid,
+    b_other,
     b_push,
     b_got,
     k_send_sem,
@@ -112,6 +114,8 @@
     ap_recv_sem,
     bp_send_sem,
     bp_recv_sem,
+    bc_send_sem,
+    bc_recv_sem,
     load_sem,
 ):
     loads = [
@@ -124,13 +128,14 @@
     wide_a, wide_b = part_a // (2 * SUBS), (width - part_a) // (2 * SUBS)
     me = lax.axis_index("exp")
     z, x, y = me // NQ, (me // NY) % NX, me % NY
-    q, r = x * NY + y, z * NY + y
+    q = x * NY + y
 
     def at(z_at, x_at, y_at):
         return {"exp": (z_at * NX + x_at) * NY + y_at}
 
     q_peers = [(q + j) % NQ for j in range(NQ)]
-    r_peers = [(r + j) % NR for j in range(NR)]
+    z_peers = [(z + j) % NZ for j in range(NZ)]
+    y_other = at(z, x, 1 - y)
     z_next = [at((z + 1) % NZ, x, y), at((z + NZ - 1) % NZ, x, y)]
     x_next = [at(z, (x + 1) % NX, y), at(z, (x + NX - 1) % NX, y)]
     ctx = lax.axis_index("ctx")
@@ -139,7 +144,7 @@
     across = {"ctx": (1 - y_lo) * 2 + core, "exp": me}
     greet(
         [at(z, p // NY, p % NY) for p in q_peers[1:]]
-        + [at(p // NY, x, p % NY) for p in r_peers[1:]]
+        + [at(p, x, y) for p in z_peers[1:]]
         + [mate, across]
     )
 
@@ -157,7 +162,7 @@
             self.copies = [
                 pltpu.make_async_remote_copy(
                     src_ref=src,
-                    dst_ref=dst.at[back, i],
+                    dst_ref=dst.at[i, back],
                     send_sem=send_sem.at[back, i],
                     recv_sem=recv_sem.at[back, i],
                     device_id=target,
@@ -165,7 +170,7 @@
                 )
                 for src, dst, send_sem, recv_sem in (
                     (
-                        keys.at[1, i]
+                        keys.at[i, 1]
                         if forward
                         else latent_ref.at[i * piece : (i + 1) * piece],
                         keys,
@@ -173,7 +178,7 @@
                         k_recv_sem,
                     ),
                     (
-                        tails.at[1, i] if forward else tail_ref.at[i],
+                        tails.at[i, 1] if forward else tail_ref.at[i],
                         tails,
                         t_send_sem,
                         t_recv_sem,
@@ -244,40 +249,43 @@
             denominator[head] = jnp.broadcast_to(mass, denominator.shape[1:])
             accum[head] = mixed
 
-    for i in range(KEY_PIECES):
-        fold(latent_ref[i * piece : (i + 1) * piece], tail_ref[i], i * piece)
-
-    def fold_from(back, i, target):
-        KeyCopy(back, i, False, target).wait_recv()
-        if back == 1:
-
-            @pl.when(core == 1)
-            def _():
-                KeyCopy(0, i, True, mate).start()
-
-        fold(keys[back, i], tails[back, i])
+    own_tail = jnp.concatenate([tail_ref[i] for i in range(KEY_PIECES)], axis=1)
+    fold(latent_ref[...], own_tail, 0)
+
+    def fold_pair(blocks):
+        block = jnp.concatenate([keys[i, back] for i, back in blocks], axis=0)
+        tail = jnp.concatenate([tails[i, back] for i, back in blocks], axis=1)
+        fold(block, tail)
+
+    def near_arrived(i):
+        KeyCopy(0, i, False, mate).wait_recv()
+
+    def far_arrived(i):
+        KeyCopy(1, i, False, across).wait_recv()
 
     @pl.when(ctx == 1)
     def _():
+        near_arrived(0)
+        near_arrived(1)
+        fold_pair(((0, 0), (1, 0)))
+
+    @pl.when(ctx == 2)
+    def _():
         for i in range(KEY_PIECES):
-            fold_from(0, i, mate)
-
-    for i in range(KEY_PIECES):
-
-        @pl.when(y_lo == 1)
-        def _():
-            fold_from(1, i, across)
-
-        if i == 0:
-
-            @pl.when(ctx == 3)
-            def _():
-                for k in range(KEY_PIECES):
-                    fold_from(0, k, mate)
-
-        @pl.when(ctx == 2)
-        def _():
-            fold_from(0, i, mate)
+            far_arrived(i)
+            near_arrived(i)
+            fold_pair(((i, 0), (i, 1)))
+
+    @pl.when(ctx == 3)
+    def _():
+        far_arrived(0)
+        KeyCopy(0, 0, True, mate).start()
+        near_arrived(0)
+        near_arrived(1)
+        fold_pair(((0, 0), (1, 0), (0, 1)))
+        far_arrived(1)
+        KeyCopy(0, 1, True, mate).start()
+        fold(keys[1, 1], tails[1, 1])
 
     for load in loads:
         load.wait()
@@ -357,25 +365,45 @@
                 )
             )
 
-    def b_push_out():
+    b_cross = []
+
+    def b_cross_out():
         for sub in range(SUBS):
             for way in range(2):
+                k = way * SUBS + sub
                 own = b_own(way, sub, x)
                 b_flight[way, sub, NX - 2].wait_recv()
                 own = own + b_slots[way, sub, NX - 2].astype(jnp.float32)
-                start = (way * SUBS + sub) * wide_b
-                b_push[:, :, start : start + wide_b] = own.reshape(
-                    NR, TOK, wide_b
-                ).astype(jnp.bfloat16)
-        for j in range(1, NR):
-            p = r_peers[j]
+                own = own.reshape(NZ, NY, TOK, wide_b)
+                for y_at in range(NY):
+                    b_mid[k, y_at] = own[:, y_at].astype(jnp.bfloat16)
+                b_cross.append(
+                    (
+                        k,
+                        remote(
+                            b_mid.at[k, 1 - y],
+                            b_other.at[k],
+                            bc_send_sem.at[k],
+                            bc_recv_sem.at[k],
+                            y_other,
+                        ),
+                    )
+                )
+
+    def b_push_out():
+        for k, copy in b_cross:
+            copy.wait_recv()
+            own = b_mid[k, y].astype(jnp.float32) + b_other[k].astype(jnp.float32)
+            b_push[:, :, k * wide_b : (k + 1) * wide_b] = own.astype(jnp.bfloat16)
+        for j in (4, 3, 5, 2, 6, 1, 7):
+            p = z_peers[j]
             pushes.append(
                 remote(
                     b_push.at[p],
                     b_got.at[j - 1],
                     bp_send_sem.at[j - 1],
                     bp_recv_sem.at[j - 1],
-                    at(p // NY, x, p % NY),
+                    at(p, x, y),
                 )
             )
 
@@ -387,21 +415,23 @@
     a_step(3)
     b_step(2)
     a_step(4)
+    b_cross_out()
+    a_step(5)
     b_push_out()
-    a_step(5)
     a_step(6)
     a_push_out()
     for copy in pushes:
         copy.wait_recv()
-    total = b_push[r].astype(jnp.float32)
-    for j in range(NR - 1):
+    total = b_push[z].astype(jnp.float32)
+    for j in range(NZ - 1):
         total = total + b_got[j].astype(jnp.float32)
     out_ref[:, part_a:] = total
     total = a_push[q].astype(jnp.float32)
     for j in range(NQ - 1):
         total = total + a_got[j].astype(jnp.float32)
     out_ref[:, :part_a] = total
-    for copy in [*a_flight.values(), *b_flight.values(), *pushes]:
+    crossed = [copy for _, copy in b_cross]
+    for copy in [*a_flight.values(), *b_flight.values(), *crossed, *pushes]:
         copy.wait_send()
     for i in range(KEY_PIECES):
 
@@ -432,8 +462,8 @@
             pltpu.VMEM(uv_weight.shape, bf16),
             pltpu.VMEM(weight.shape, bf16),
             pltpu.VMEM((KEY_PIECES, ROPE + DOC_ROWS, rows // KEY_PIECES), bf16),
-            pltpu.VMEM((2, KEY_PIECES, rows // KEY_PIECES, lat), bf16),
-            pltpu.VMEM((2, KEY_PIECES, ROPE + DOC_ROWS, rows // KEY_PIECES), bf16),
+            pltpu.VMEM((KEY_PIECES, 2, rows // KEY_PIECES, lat), bf16),
+            pltpu.VMEM((KEY_PIECES, 2, ROPE + DOC_ROWS, rows // KEY_PIECES), bf16),
             pltpu.VMEM((heads, rows, 128), jnp.float32),
             pltpu.VMEM((heads, rows, 128), jnp.float32),
             pltpu.VMEM((heads, rows, lat), jnp.float32),
@@ -444,8 +474,10 @@
             pltpu.VMEM((2, SUBS, NX - 1, NR * TOK, wide_b), bf16),
             pltpu.VMEM((NQ, TOK, part_a), bf16),
             pltpu.VMEM((NQ - 1, TOK, part_a), bf16),
-            pltpu.VMEM((NR, TOK, part_b), bf16),
-            pltpu.VMEM((NR - 1, TOK, part_b), bf16),
+            pltpu.VMEM((2 * SUBS, NY, NZ, TOK, wide_b), bf16),
+            pltpu.VMEM((2 * SUBS, NZ, TOK, wide_b), bf16),
+            pltpu.VMEM((NZ, TOK, part_b), bf16),
+            pltpu.VMEM((NZ - 1, TOK, part_b), bf16),
             dma((2, KEY_PIECES)),
             dma((2, KEY_PIECES)),
             dma((2, KEY_PIECES)),
@@ -456,8 +488,10 @@
             dma((2, SUBS, NX - 1)),
             dma((NQ - 1,)),
             dma((NQ - 1,)),
-            dma((NR - 1,)),
-            dma((NR - 1,)),
+            dma((NZ - 1,)),
+            dma((NZ - 1,)),
+            dma((2 * SUBS,)),
+            dma((2 * SUBS,)),
             dma((2,)),
         ],
         compiler_params=pltpu.CompilerParams(
@@ -469,8 +503,6 @@
 
 def experts_kernel(
     rows_ref,
-    state_ref,
-    scale_ref,
     gate_hbm,
     up_hbm,
     down_hbm,
@@ -515,7 +547,7 @@
     h_send,
     h_recv,
 ):
-    width = state_ref.shape[1]
+    width = down_hbm.shape[1]
     sent = width + 2 * N_EXPERTS
     half_rows, half_slots = NZ * TOK, NQ * NZ * CAP
     piece = NZ * CAP
@@ -758,13 +790,13 @@
     total = to_z[z].astype(jnp.float32)
     for j in range(NZ - 1):
         total = total + from_z[j].astype(jnp.float32)
-    out_ref[...] = (state_ref[...] + total * scale_ref[:, :1]).astype(jnp.bfloat16)
+    out_ref[...] = total
     for copy in pending:
         copy.wait_send()
 
 
-def run_experts(rows, state, scale, gate, up, down):
-    width = state.shape[1]
+def run_experts(rows, gate, up, down):
+    width = down.shape[1]
     sent = width + 2 * N_EXPERTS
     half_slots, piece = NQ * NZ * CAP, NZ * CAP
     bf16, f32 = jnp.bfloat16, jnp.float32
@@ -774,10 +806,10 @@
     return pl.pallas_call(
         experts_kernel,
         out_shape=(
-            jax.ShapeDtypeStruct((TOK, width), bf16),
+            jax.ShapeDtypeStruct((TOK, width), f32),
             jax.ShapeDtypeStruct((8, 2 * N_EXPERTS), f32),
         ),
-        in_specs=[vmem, vmem, vmem, hbm, hbm, hbm],
+        in_specs=[vmem, hbm, hbm, hbm],
         out_specs=(vmem, vmem),
         scratch_shapes=[
             pltpu.VMEM(gate.shape, bf16),
@@ -823,7 +855,7 @@
             collective_id=1, has_side_effects=True, vmem_limit_bytes=60 << 20
         ),
         name="experts",
-    )(rows, state, scale, gate, up, down)
+    )(rows, gate, up, down)
 
 
 def route_lanes(expert_ids, gate_levels, bin_ids):
@@ -875,15 +907,9 @@
     rows = jnp.concatenate(
         (normed, route_lanes(expert_ids, gate_levels, bin_ids)), axis=1
     )
+    mixture, hist = run_experts(rows, gate_weight[0], up_weight[0], down_weight[0])
     scale = 1.0 / jnp.sum(gate_levels.astype(jnp.float32), axis=1, keepdims=True)
-    layer_out, hist = run_experts(
-        rows,
-        stream_state,
-        jnp.broadcast_to(scale, (TOK, 128)),
-        gate_weight[0],
-        up_weight[0],
-        down_weight[0],
-    )
+    layer_out = (stream_state + mixture * scale).astype(jnp.bfloat16)
     histogram = hist[:, : NBINS // 32].reshape(1, NBINS // N_CTX)
     return (layer_out, histogram)
 

time: 177 us -> 168 us (0.949)
  Pallas kernels: 168 us -> 158 us
  other arithmetic: 1.49 us -> 3.99 us
  local copies, waits for them, and re-layouts: 6.65 us -> 4.53 us
    pallas_call x1, Pallas kernels: 63.5 us -> 57.5 us  [attend_sum(): pl.pallas_call(functools.partial(attend_sum_kernel, part_a), out_shape=ja...]
    pallas_call x1, Pallas kernels: 105 us -> 100 us  [run_experts(): pl.pallas_call(experts_kernel, out_shape=(jax.ShapeDtypeStruct((TOK, widt...]
    unnamed x14 -> x13, local copies, waits for them, and re-layouts: 3.93 us -> 2.49 us
where the time goes in v5:
time: 168 us; the launch traced here: 167 us
  Pallas kernels  158 us (94%)
  local copies, waits for them, and re-layouts  4.53 us (3%)
  other arithmetic  3.99 us (2%)
    pallas_call x1, Pallas kernels, run_experts(): pl.pallas_call(experts_kernel, out_shape=(jax.ShapeDtypeStruct((TOK, widt...  100 us
    pallas_call x1, Pallas kernels, attend_sum(): pl.pallas_call(functools.partial(attend_sum_kernel, part_a), out_shape=ja...  57.5 us

profile of v5, /device:TPU:1, one launch (start us, length us, event | category | flops | bytes accessed | tf_op | source)
XLA Modules:
  0.0 167.3 jit_solution(2722657916522402764)
XLA Ops:
  0.6 2.5 %copy.17 = bf16[64,8,2,512]{3,1,2,0:T(8,128)(2,1)} copy(bf16[64,8,2,512]{3,2,1,0:T(2,128)(2,1)} %bitcast.12) | data formatting | bytes 2097152
  3.1 0.0 copy-start.1
  3.1 0.0 copy-start.3
  3.1 0.0 copy-start.4
  3.1 0.0 copy-start.2
  3.1 0.0 copy-start.5
  3.1 57.5 %attend_sum.1 = f32[8,3584]{1,0:T(8,128)} custom-call(bf16[512,1024]{1,0:T(8,128)(2,1)} %bitcast.8, bf16[512,128]{1,0:T(8,128)(2,1)} %query_rope_ref.1, bf16[512,512]{1,0:T(8,128)(2,1)} %latent_ref.1, bf16[64,512]{1,0:T(8,128)(2,1)} %bitcast.13, s32[1,512]{1,0:T(1,128)} %bitcast.15, bf16[2,512,128]{2,1,0:T(8,128)(2,1)} %uv_hbm.1, bf16[256,3584]{1,0:T(8,128)(2,1)} %weight_hbm.1), custom_call_target="tpu_custom_call" | custom-call | tf_op jit(solution)/shard_map/attend_sum/pallas_call | solution.py:455
  60.6 0.0 copy-done.1
  60.6 1.0 multiply_reduce_fusion
  61.7 0.0 copy-done.3
  61.7 1.0 multiply_convert_fusion
  62.7 0.0 copy-done.4
  62.7 0.0 copy-done.2
  62.7 0.0 copy-done.5
  62.7 0.1 convert_reduce_fusion
  62.9 0.1 select_reduce_fusion
  63.0 0.7 concatenate.6.rows_ref
  63.7 0.0 copy-start
  63.7 100.5 %experts.1 = (f32[8,3584]{1,0:T(8,128)}, f32[8,128]{1,0:T(8,128)}) custom-call(bf16[8,3840]{1,0:T(8,128)(2,1)} %concatenate.6.rows_ref, bf16[3584,256]{1,0:T(8,128)(2,1)} %bitcast.9, bf16[3584,256]{1,0:T(8,128)(2,1)} %bitcast.10, bf16[256,3584]{1,0:T(8,128)(2,1)} %bitcast.11), custom_call_target="tpu_custom_call" | custom-call | tf_op jit(solution)/shard_map/experts/pallas_call | solution.py:806
  164.2 0.1 convert_reduce_fusion.1
  164.3 0.0 copy-done
  164.3 1.6 add_convert_fusion
  165.9 1.3 reshape.45
  (8 shorter events, 0.1 us)
Async XLA Ops:
  3.1 57.5 %copy-start.1 = (bf16[8,3584]{1,0:T(8,128)(2,1)S(1)}, bf16[8,3584]{1,0:T(8,128)(2,1)}, u32[]{:S(2)}) copy-start(bf16[8,3584]{1,0:T(8,128)(2,1)} %param.15) | copy-start | bytes 172036
  3.1 58.6 %copy-start.3 = (f32[3584]{0:T(1024)S(1)}, f32[3584]{0:T(1024)}, u32[]{:S(2)}) copy-start(f32[3584]{0:T(1024)} %param.16) | copy-start | bytes 43012
  3.1 59.6 %copy-start.4 = (s32[8,8]{1,0:T(8,128)S(1)}, s32[8,8]{1,0:T(8,128)}, u32[]{:S(2)}) copy-start(s32[8,8]{1,0:T(8,128)} %param.26) | copy-start | bytes 772
  3.1 59.6 %copy-start.2 = (s32[8,8]{1,0:T(8,128)S(1)}, s32[8,8]{1,0:T(8,128)}, u32[]{:S(2)}) copy-start(s32[8,8]{1,0:T(8,128)} %param.25) | copy-start | bytes 772
  3.1 59.6 %copy-start.5 = (s32[8,8]{1,0:T(8,128)S(1)}, s32[8,8]{1,0:T(8,128)}, u32[]{:S(2)}) copy-start(s32[8,8]{1,0:T(8,128)} %param.24) | copy-start | bytes 772
  63.7 100.6 %copy-start = (f32[8,3584]{1,0:T(8,128)S(1)}, f32[8,3584]{1,0:T(8,128)}, u32[]{:S(2)}) copy-start(f32[8,3584]{1,0:T(8,128)} %attend_sum.1) | copy-start | bytes 344068

commit v6 on v5

--- a/solution.py
+++ b/solution.py
@@ -85,6 +85,7 @@
     out_ref,
     uv_ref,
     weight_ref,
+    nope_ref,
     tail_ref,
     keys,
     tails,
@@ -216,6 +217,15 @@
         )
 
     heads = uv_ref.shape[0]
+    part = block_len // 8
+
+    def unpack(i, carry):
+        here = pl.ds(pl.multiple_of(i * part, part), part)
+        for head in range(heads):
+            nope_ref[head, here] = query_ref[here, head]
+        return carry
+
+    lax.fori_loop(0, 8, unpack, 0)
     doc_pick = small(lax.broadcasted_iota(jnp.int32, (DOC_ROWS, 128), 0) == 0)
     query_docs = jnp.concatenate(
         [mm_t(tail_ref[i, ROPE:], doc_pick)[:, :1] for i in range(KEY_PIECES)], axis=0
@@ -230,7 +240,7 @@
             key_at = lax.broadcasted_iota(jnp.int32, shape, 1) + offset
             allowed = allowed & (key_at <= query_at)
         for head in range(heads):
-            nope = query_ref[:, head * lat : (head + 1) * lat]
+            nope = nope_ref[head]
             rope = query_rope_ref[:, head * ROPE : (head + 1) * ROPE]
             raw = nt(nope, block) + mm(rope, tail[:ROPE])
             scores = jnp.where(allowed, raw, masked_score)
@@ -461,6 +471,7 @@
         scratch_shapes=[
             pltpu.VMEM(uv_weight.shape, bf16),
             pltpu.VMEM(weight.shape, bf16),
+            pltpu.VMEM((heads, rows, lat), bf16),
             pltpu.VMEM((KEY_PIECES, ROPE + DOC_ROWS, rows // KEY_PIECES), bf16),
             pltpu.VMEM((KEY_PIECES, 2, rows // KEY_PIECES, lat), bf16),
             pltpu.VMEM((KEY_PIECES, 2, ROPE + DOC_ROWS, rows // KEY_PIECES), bf16),
@@ -655,36 +666,19 @@
             p = (q + j) % NQ
             slot_flight[half, j] = remote(
                 slots.at[half, p],
-                inbox.at[0, half, q],
+                inbox.at[half, 0, q],
                 q_send.at[half, j],
                 q_recv.at[half, j],
                 q_peer(p),
             )
-        inbox[0, half, q] = slots[half, q]
+        inbox[half, 0, q] = slots[half, q]
     pending += slot_flight.values()
-
-    mate_flight = []
-    for half in range(2):
-        for j in (0,) + q_order:
-            q_from = (q + NQ - j) % NQ
-            if j:
-                slot_flight[half, j].wait_recv()
-            mate_flight.append(
-                remote(
-                    inbox.at[0, half, q_from],
-                    inbox.at[1, half, q_from],
-                    m_send.at[half, j],
-                    m_recv.at[half, j],
-                    mate,
-                )
-            )
-    pending += mate_flight
 
     bin_lane = lax.broadcasted_iota(jnp.int32, (2 * half_slots, 2 * N_EXPERTS), 1)
     bins_at = bin_lane.astype(jnp.float32)
 
-    def run_block(which):
-        block = inbox[which].reshape(2 * half_slots, sent)
+    def run_block(half):
+        block = inbox[half].reshape(2 * half_slots, sent)
         x = block[:, :width]
         gate_part, up_part = mm(x, gate_ref[...]), mm(x, up_ref[...])
         activation = gate_part / (1.0 + jnp.exp(-gate_part)) * up_part
@@ -700,42 +694,42 @@
         hist = mm_t(first, at_low) + mm_t(second, at_low) + mm_t(third, at_low)
         return activation.astype(jnp.bfloat16), hist
 
-    for load in loads:
-        load.wait()
-    hidden, hist = run_block(0)
-    kept[...] = mm(hidden, down_ref[...])
-    for copy in mate_flight:
-        copy.wait_recv()
-    hidden, more = run_block(1)
-    to_mate[...] = (
-        mm(hidden, down_ref[...]).astype(jnp.bfloat16).reshape(to_mate.shape)
-    )
-    mate_out = {}
-    for half in (1, 0):
-        mate_out[half] = remote(
+    back_flight = {}
+
+    def run_half(half):
+        flight = []
+        for j in (0,) + q_order:
+            q_from = (q + NQ - j) % NQ
+            if j:
+                slot_flight[half, j].wait_recv()
+            flight.append(
+                remote(
+                    inbox.at[half, 0, q_from],
+                    inbox.at[half, 1, q_from],
+                    m_send.at[half, j],
+                    m_recv.at[half, j],
+                    mate,
+                )
+            )
+        for copy in flight:
+            copy.wait_recv()
+        if half == 0:
+            for load in loads:
+                load.wait()
+        hidden, hist = run_block(half)
+        to_mate[half] = (
+            mm(hidden[half_slots:], down_ref[...])
+            .astype(jnp.bfloat16)
+            .reshape(NQ, piece, width)
+        )
+        swap = remote(
             to_mate.at[half], from_mate.at[half], o_send.at[half], o_recv.at[half], mate
         )
-    pending += mate_out.values()
-
-    hist_out[...] = (hist + more)[: N_CTX * 8].reshape(N_CTX, 8, 2 * N_EXPERTS)
-    hist_flight = [
-        remote(
-            hist_out.at[(ctx + j) % N_CTX],
-            hist_in.at[j - 1],
-            h_send.at[j - 1],
-            h_recv.at[j - 1],
-            c_peer(j),
-        )
-        for j in range(1, N_CTX)
-    ]
-    pending += hist_flight
-
-    back_flight = {}
-    for half in (1, 0):
-        mate_out[half].wait_recv()
-        total = kept[half * half_slots : (half + 1) * half_slots] + from_mate[
-            half
-        ].reshape(half_slots, width).astype(jnp.float32)
+        kept[...] = mm(hidden[:half_slots], down_ref[...])
+        swap.wait_recv()
+        total = kept[...] + from_mate[half].reshape(half_slots, width).astype(
+            jnp.float32
+        )
         back[half] = total.astype(jnp.bfloat16).reshape(NQ, piece, width)
         for j in q_order:
             p = (q + j) % NQ
@@ -747,6 +741,25 @@
                 q_peer(p),
             )
         returned[half, q] = back[half, q]
+        pending.extend(flight + [swap])
+        return hist
+
+    hist = run_half(0)
+    more = run_half(1)
+
+    hist_out[...] = (hist + more)[: N_CTX * 8].reshape(N_CTX, 8, 2 * N_EXPERTS)
+    hist_flight = [
+        remote(
+            hist_out.at[(ctx + j) % N_CTX],
+            hist_in.at[j - 1],
+            h_send.at[j - 1],
+            h_recv.at[j - 1],
+            c_peer(j),
+        )
+        for j in range(1, N_CTX)
+    ]
+    pending += hist_flight
+
     pending += back_flight.values()
 
     def mixed(half):
@@ -754,6 +767,7 @@
             back_flight[half, j].wait_recv()
         return mm(weigh[half], returned[half].reshape(half_slots, width))
 
+    own[...] = mixed(0).reshape(NZ, TOK, width)
     to_y[...] = mixed(1).reshape(NZ, TOK, width).astype(jnp.bfloat16)
     y_flight = {}
     for j in order + (0,):
@@ -762,7 +776,6 @@
             to_y.at[z_to], from_y.at[z_to], ys_send.at[j], ys_recv.at[j], y_peer
         )
     pending += y_flight.values()
-    own[...] = mixed(0).reshape(NZ, TOK, width)
     z_flight = []
     for j in order + (0,):
         z_to = (z + j) % NZ
@@ -819,7 +832,7 @@
             pltpu.VMEM((2, NZ * TOK, half_slots), bf16),
             pltpu.VMEM((2, NQ, piece, sent), bf16),
             pltpu.VMEM((2, 2, NQ, piece, sent), bf16),
-            pltpu.VMEM((2 * half_slots, width), f32),
+            pltpu.VMEM((half_slots, width), f32),
             pltpu.VMEM((2, NQ, piece, width), bf16),
             pltpu.VMEM((2, NQ, piece, width), bf16),
             pltpu.VMEM((2, NQ, piece, width), bf16),
@@ -888,9 +901,9 @@
     up_weight,
     down_weight,
 ):
-    block_len, head_count, _ = q_nope.shape
+    block_len = q_nope.shape[0]
     attended = attend_sum(
-        q_nope.reshape(block_len, head_count * q_nope.shape[2]),
+        q_nope,
         q_rope,
         latent,
         k_rope.T,

time: 168 us -> 161 us (0.958)
  Pallas kernels: 158 us -> 152 us
  local copies, waits for them, and re-layouts: 4.53 us -> 2.06 us
    pallas_call x1, Pallas kernels: 100 us -> 92.7 us  [run_experts(): pl.pallas_call(experts_kernel, out_shape=(jax.ShapeDtypeStruct((TOK, widt...]
    unnamed x13 -> x8, local copies, waits for them, and re-layouts: 2.49 us -> 0.02 us
    pallas_call x1, Pallas kernels: 57.5 us -> 59.4 us  [attend_sum(): pl.pallas_call(functools.partial(attend_sum_kernel, part_a), out_shape=ja...]
where the time goes in v6:
time: 161 us; the launch traced here: 160 us
  Pallas kernels  152 us (94%)
  other arithmetic  5.38 us (3%)
  local copies, waits for them, and re-layouts  2.06 us (1%)
    pallas_call x1, Pallas kernels, run_experts(): pl.pallas_call(experts_kernel, out_shape=(jax.ShapeDtypeStruct((TOK, widt...  92.7 us
    pallas_call x1, Pallas kernels, attend_sum(): pl.pallas_call(functools.partial(attend_sum_kernel, part_a), out_shape=ja...  59.4 us

profile of v6, /device:TPU:1, one launch (start us, length us, event | category | flops | bytes accessed | tf_op | source)
XLA Modules:
  0.0 160.3 jit_solution(16926606695518748434)
XLA Ops:
  0.6 0.7 add_select_fusion.1
  1.3 0.8 convert_reduce_fusion
  2.2 0.1 select_reduce_fusion
  2.3 0.0 copy-start.1
  2.3 0.0 copy-start.3
  2.3 59.4 %attend_sum.1 = f32[8,3584]{1,0:T(8,128)} custom-call(bf16[512,2,512]{2,1,0:T(2,128)(2,1)} %query_ref.1, bf16[512,128]{1,0:T(8,128)(2,1)} %query_rope_ref.1, bf16[512,512]{1,0:T(8,128)(2,1)} %latent_ref.1, bf16[64,512]{1,0:T(8,128)(2,1)} %bitcast.9, s32[1,512]{1,0:T(1,128)} %bitcast.11, bf16[2,512,128]{2,1,0:T(8,128)(2,1)} %uv_hbm.1, ...), custom_call_target="tpu_custom_call" | custom-call | tf_op jit(solution)/shard_map/attend_sum/pallas_call | solution.py:465
  61.8 0.0 copy-done.1
  61.8 1.0 multiply_reduce_fusion
  62.8 0.0 copy-done.3
  62.8 1.0 multiply_convert_fusion
  63.8 0.7 concatenate.6.rows_ref
  64.5 0.0 copy-start.2
  64.5 0.0 copy-start
  64.5 92.7 %experts.1 = (f32[8,3584]{1,0:T(8,128)}, f32[8,128]{1,0:T(8,128)}) custom-call(bf16[8,3840]{1,0:T(8,128)(2,1)} %concatenate.6.rows_ref, bf16[3584,256]{1,0:T(8,128)(2,1)} %bitcast.6, bf16[3584,256]{1,0:T(8,128)(2,1)} %bitcast.7, bf16[256,3584]{1,0:T(8,128)(2,1)} %bitcast.8), custom_call_target="tpu_custom_call" | custom-call | tf_op jit(solution)/shard_map/experts/pallas_call | solution.py:819
  157.2 0.0 copy-done.2
  157.2 0.1 convert_reduce_fusion.1
  157.4 0.0 copy-done
  157.4 1.6 add_convert_fusion
  159.0 1.3 reshape.41
  (7 shorter events, 0.0 us)
Async XLA Ops:
  2.3 59.5 %copy-start.1 = (bf16[8,3584]{1,0:T(8,128)(2,1)S(1)}, bf16[8,3584]{1,0:T(8,128)(2,1)}, u32[]{:S(2)}) copy-start(bf16[8,3584]{1,0:T(8,128)(2,1)} %param.15) | copy-start | bytes 172036
  2.3 60.5 %copy-start.3 = (f32[3584]{0:T(1024)S(1)}, f32[3584]{0:T(1024)}, u32[]{:S(2)}) copy-start(f32[3584]{0:T(1024)} %param.16) | copy-start | bytes 43012
  64.5 92.7 %copy-start.2 = (s32[8,8]{1,0:T(8,128)S(1)}, s32[8,8]{1,0:T(8,128)}, u32[]{:S(2)}) copy-start(s32[8,8]{1,0:T(8,128)} %param.25) | copy-start | bytes 772
  64.5 92.8 %copy-start = (f32[8,3584]{1,0:T(8,128)S(1)}, f32[8,3584]{1,0:T(8,128)}, u32[]{:S(2)}) copy-start(f32[8,3584]{1,0:T(8,128)} %attend_sum.1) | copy-start | bytes 344068

commit v7 on v6

--- a/solution.py
+++ b/solution.py
@@ -146,7 +146,7 @@
     greet(
         [at(z, p // NY, p % NY) for p in q_peers[1:]]
         + [at(p, x, y) for p in z_peers[1:]]
-        + [mate, across]
+        + [mate, across, {"ctx": 3 - ctx, "exp": me}]
     )
 
     block_len, lat = latent_ref.shape
@@ -454,7 +454,7 @@
             KeyCopy(0, i, False, mate).wait_send()
 
 
-def attend_sum(q_nope, q_rope, latent, rope_t, docs, uv_weight, weight, part_a=2048):
+def attend_scratch(latent, uv_weight, weight, part_a):
     heads, lat = uv_weight.shape[:2]
     rows = latent.shape[0]
     width = weight.shape[1]
@@ -462,13 +462,7 @@
     wide_a, wide_b = part_a // (2 * SUBS), part_b // (2 * SUBS)
     bf16 = jnp.bfloat16
     dma = pltpu.SemaphoreType.DMA
-    return pl.pallas_call(
-        functools.partial(attend_sum_kernel, part_a),
-        out_shape=jax.ShapeDtypeStruct((TOK, width), jnp.float32),
-        in_specs=[pl.BlockSpec(memory_space=pltpu.VMEM)] * 5
-        + [pl.BlockSpec(memory_space=pltpu.HBM)] * 2,
-        out_specs=pl.BlockSpec(memory_space=pltpu.VMEM),
-        scratch_shapes=[
+    return [
             pltpu.VMEM(uv_weight.shape, bf16),
             pltpu.VMEM(weight.shape, bf16),
             pltpu.VMEM((heads, rows, lat), bf16),
@@ -504,12 +498,15 @@
             dma((2 * SUBS,)),
             dma((2 * SUBS,)),
             dma((2,)),
-        ],
-        compiler_params=pltpu.CompilerParams(
-            collective_id=0, has_side_effects=True, vmem_limit_bytes=60 << 20
-        ),
-        name="attend_sum",
-    )(q_nope, q_rope, latent, rope_t, docs, uv_weight, weight)
+    ]
+
+
+def expert_loads(gate_hbm, up_hbm, down_hbm, gate_ref, up_ref, down_ref, load_sem):
+    return [
+        pltpu.make_async_copy(gate_hbm, gate_ref, load_sem.at[0]),
+        pltpu.make_async_copy(up_hbm, up_ref, load_sem.at[1]),
+        pltpu.make_async_copy(down_hbm, down_ref, load_sem.at[2]),
+    ]
 
 
 def experts_kernel(
@@ -578,18 +575,8 @@
     def c_peer(j):
         return {"ctx": (ctx + j) % N_CTX, "exp": me}
 
-    loads = [
-        pltpu.make_async_copy(src, dst, load_sem.at[i])
-        for i, (src, dst) in enumerate(
-            ((gate_hbm, gate_ref), (up_hbm, up_ref), (down_hbm, down_ref))
-        )
-    ]
-    for load in loads:
-        load.start()
-    greet(
-        [z_peer((z + j) % NZ) for j in range(1, NZ)]
-        + [q_peer((q + j) % NQ) for j in range(1, NQ)]
-        + [c_peer(j) for j in range(1, N_CTX)]
+    loads = expert_loads(
+        gate_hbm, up_hbm, down_hbm, gate_ref, up_ref, down_ref, load_sem
     )
     pending = []
 
@@ -808,27 +795,17 @@
         copy.wait_send()
 
 
-def run_experts(rows, gate, up, down):
+def expert_scratch(gate, up, down):
     width = down.shape[1]
     sent = width + 2 * N_EXPERTS
     half_slots, piece = NQ * NZ * CAP, NZ * CAP
     bf16, f32 = jnp.bfloat16, jnp.float32
     dma = pltpu.SemaphoreType.DMA
-    vmem = pl.BlockSpec(memory_space=pltpu.VMEM)
-    hbm = pl.BlockSpec(memory_space=pltpu.HBM)
-    return pl.pallas_call(
-        experts_kernel,
-        out_shape=(
-            jax.ShapeDtypeStruct((TOK, width), f32),
-            jax.ShapeDtypeStruct((8, 2 * N_EXPERTS), f32),
-        ),
-        in_specs=[vmem, hbm, hbm, hbm],
-        out_specs=(vmem, vmem),
-        scratch_shapes=[
+    return [
             pltpu.VMEM(gate.shape, bf16),
             pltpu.VMEM(up.shape, bf16),
             pltpu.VMEM(down.shape, bf16),
-            pltpu.VMEM((2, NZ, TOK, rows.shape[1]), bf16),
+            pltpu.VMEM((2, NZ, TOK, sent + 2 * N_EXPERTS), bf16),
             pltpu.VMEM((2, NZ * TOK, half_slots), bf16),
             pltpu.VMEM((2, NQ, piece, sent), bf16),
             pltpu.VMEM((2, 2, NQ, piece, sent), bf16),
@@ -863,25 +840,79 @@
             dma((NZ - 1,)),
             dma((N_CTX - 1,)),
             dma((N_CTX - 1,)),
+    ]
+
+
+def fill_lanes(ids_ref, levels_ref, bins_ref, rows_ref, width):
+    expert = lax.broadcasted_iota(jnp.int32, (TOK, N_EXPERTS), 1)
+    none = jnp.zeros((TOK, N_EXPERTS), jnp.int32)
+    high, low, level, named = none, none, none, none
+    for k in range(ids_ref.shape[1]):
+        here = ids_ref[:, k : k + 1] == expert
+        bins = bins_ref[:, k : k + 1]
+        high = high + jnp.where(here, bins >> 6, 0)
+        low = low + jnp.where(here, bins & 63, 0)
+        level = level + jnp.where(here, levels_ref[:, k : k + 1], 0)
+        named = named + jnp.where(here, 1, 0)
+    row = lax.broadcasted_iota(jnp.int32, (TOK, N_EXPERTS), 0)
+    rank = none
+    for t in range(TOK - 1):
+        rank = rank + jnp.where(row > t, named[t : t + 1], 0)
+    for i, lanes in enumerate((high, low, level, rank)):
+        rows_ref[:, width + i * N_EXPERTS : width + (i + 1) * N_EXPERTS] = lanes.astype(
+            jnp.float32
+        ).astype(jnp.bfloat16)
+
+
+def layer_kernel(part_a, attend_count, *refs):
+    attend_in, (residual, gain, ids, levels, bins), weights = (
+        refs[:7],
+        refs[7:12],
+        refs[12:15],
+    )
+    state_out, mixture_out, hist_out = refs[15:18]
+    attended, rows = refs[18:20]
+    attend_refs = refs[20 : 20 + attend_count]
+    expert_refs = refs[20 + attend_count :]
+    for load in expert_loads(*weights, *expert_refs[:3], expert_refs[19]):
+        load.start()
+    width = residual.shape[1]
+    fill_lanes(ids, levels, bins, rows, width)
+    attend_sum_kernel(part_a, *attend_in, attended, *attend_refs)
+    state = residual[...].astype(jnp.float32) + attended[...]
+    state_out[...] = state
+    mean = jnp.mean(state * state, axis=1, keepdims=True)
+    rows[:, :width] = (state * lax.rsqrt(mean + norm_eps) * gain[...]).astype(
+        jnp.bfloat16
+    )
+    experts_kernel(rows, *weights, mixture_out, hist_out, *expert_refs)
+
+
+def run_layer(attend_in, uv_weight, weight, row_in, gate, up, down, part_a=2048):
+    width = weight.shape[1]
+    vmem = pl.BlockSpec(memory_space=pltpu.VMEM)
+    hbm = pl.BlockSpec(memory_space=pltpu.HBM)
+    attend_refs = attend_scratch(attend_in[2], uv_weight, weight, part_a)
+    return pl.pallas_call(
+        functools.partial(layer_kernel, part_a, len(attend_refs)),
+        out_shape=(
+            jax.ShapeDtypeStruct((TOK, width), jnp.float32),
+            jax.ShapeDtypeStruct((TOK, width), jnp.float32),
+            jax.ShapeDtypeStruct((8, 2 * N_EXPERTS), jnp.float32),
+        ),
+        in_specs=[vmem] * 5 + [hbm] * 2 + [vmem] * 5 + [hbm] * 3,
+        out_specs=(vmem, vmem, vmem),
+        scratch_shapes=[
+            pltpu.VMEM((TOK, width), jnp.float32),
+            pltpu.VMEM((TOK, width + 4 * N_EXPERTS), jnp.bfloat16),
+            *attend_refs,
+            *expert_scratch(gate, up, down),
         ],
         compiler_params=pltpu.CompilerParams(
-            collective_id=1, has_side_effects=True, vmem_limit_bytes=60 << 20
+            collective_id=0, has_side_effects=True, vmem_limit_bytes=60 << 20
         ),
-        name="experts",
-    )(rows, gate, up, down)
-
-
-def route_lanes(expert_ids, gate_levels, bin_ids):
-    onehot = expert_ids[:, :, None] == jnp.arange(N_EXPERTS, dtype=jnp.int32)
-
-    def spread(v):
-        return jnp.sum(jnp.where(onehot, v[:, :, None], 0), axis=1)
-
-    named = jnp.sum(onehot.astype(jnp.int32), axis=1)
-    earlier = jnp.arange(TOK)[:, None] > jnp.arange(TOK)[None, :]
-    rank = jnp.sum(jnp.where(earlier[:, :, None], named[None, :, :], 0), axis=1)
-    lanes = (spread(bin_ids // 64), spread(bin_ids % 64), spread(gate_levels), rank)
-    return jnp.concatenate(lanes, axis=1).astype(jnp.bfloat16)
+        name="layer",
+    )(*attend_in, uv_weight, weight, *row_in, gate, up, down)
 
 
 def on_device(
@@ -902,25 +933,15 @@
     down_weight,
 ):
     block_len = q_nope.shape[0]
-    attended = attend_sum(
-        q_nope,
-        q_rope,
-        latent,
-        k_rope.T,
-        doc_ids.reshape(1, block_len),
+    stream_state, mixture, hist = run_layer(
+        (q_nope, q_rope, latent, k_rope.T, doc_ids.reshape(1, block_len)),
         uv_weight,
         out_weight,
+        (residual_in, norm_gain[None], expert_ids, gate_levels, bin_ids),
+        gate_weight[0],
+        up_weight[0],
+        down_weight[0],
     )
-    stream_state = residual_in.astype(jnp.float32) + attended
-    normed = (
-        stream_state
-        * lax.rsqrt(jnp.mean(stream_state * stream_state, axis=1, keepdims=True) + norm_eps)
-        * norm_gain
-    ).astype(jnp.bfloat16)
-    rows = jnp.concatenate(
-        (normed, route_lanes(expert_ids, gate_levels, bin_ids)), axis=1
-    )
-    mixture, hist = run_experts(rows, gate_weight[0], up_weight[0], down_weight[0])
     scale = 1.0 / jnp.sum(gate_levels.astype(jnp.float32), axis=1, keepdims=True)
     layer_out = (stream_state + mixture * scale).astype(jnp.bfloat16)
     histogram = hist[:, : NBINS // 32].reshape(1, NBINS // N_CTX)

time: 161 us -> 153 us (0.950); the launches traced: 160 us -> 150 us
  Pallas kernels: 152 us -> 145 us
  other arithmetic: 5.38 us -> 2.47 us
    pallas_call x2 -> x1, Pallas kernels: 152 us -> 145 us  [run_layer(): pl.pallas_call(functools.partial(layer_kernel, part_a, len(attend_refs)),...]
    reduce_sum x3 -> x0, other arithmetic: 1.95 us -> none  [the longest x1 1.04 us: on_device(): jnp.mean(stream_state * stream_state, axis=1, keepdims=True) + norm_eps]
where the time goes in v7:
time: 153 us; the launch traced here: 150 us
  Pallas kernels  145 us (95%)
  local copies, waits for them, and re-layouts  2.66 us (2%)
  other arithmetic  2.47 us (2%)
    pallas_call x1, Pallas kernels, run_layer(): pl.pallas_call(functools.partial(layer_kernel, part_a, len(attend_refs)),...  145 us

profile of v7, /device:TPU:1, one launch (start us, length us, event | category | flops | bytes accessed | tf_op | source)
XLA Modules:
  0.0 150.5 jit_solution(1147010630845872954)
XLA Ops:
  0.6 0.8 convert_reduce_fusion
  1.4 1.3 broadcast_in_dim.4.refs_8_
  2.8 144.7 %layer.1 = (f32[8,3584]{1,0:T(8,128)}, f32[8,3584]{1,0:T(8,128)}, f32[8,128]{1,0:T(8,128)}) custom-call(bf16[512,2,512]{2,1,0:T(2,128)(2,1)} %refs_0_.1, bf16[512,128]{1,0:T(8,128)(2,1)} %refs_1_.1, bf16[512,512]{1,0:T(8,128)(2,1)} %refs_2_.1, bf16[64,512]{1,0:T(8,128)(2,1)} %bitcast.9, s32[1,512]{1,0:T(1,128)} %bitcast.11, bf16[2,512,128]{2,1,0:T(8,128)(2,1)} %refs_5_.1, ...), custom_call_target="tpu_custom_call" | custom-call | tf_op jit(solution)/shard_map/layer/pallas_call | solution.py:896
  147.5 1.7 %add_convert_fusion = bf16[8,3584]{1,0:T(8,128)(2,1)} fusion(f32[8,3584]{1,0:T(8,128)} %get-tuple-element.5, f32[8,3584]{1,0:T(8,128)} %get-tuple-element.6, f32[8]{0:T(128)S(1)} %broadcast_divide_fusion), kind=kLoop, calls=%fused_computation | loop fusion | flops 86016 | bytes 286752 | tf_op jit(solution)/shard_map/convert_element_type | solution.py:946
  149.2 1.3 reshape.15
  (1 shorter events, 0.0 us)

commit v8 on v7

--- a/solution.py
+++ b/solution.py
@@ -870,8 +870,8 @@
         refs[7:12],
         refs[12:15],
     )
-    state_out, mixture_out, hist_out = refs[15:18]
-    attended, rows = refs[18:20]
+    layer_out, hist_out = refs[15:17]
+    attended, mixture, rows = refs[17:20]
     attend_refs = refs[20 : 20 + attend_count]
     expert_refs = refs[20 + attend_count :]
     for load in expert_loads(*weights, *expert_refs[:3], expert_refs[19]):
@@ -880,12 +880,14 @@
     fill_lanes(ids, levels, bins, rows, width)
     attend_sum_kernel(part_a, *attend_in, attended, *attend_refs)
     state = residual[...].astype(jnp.float32) + attended[...]
-    state_out[...] = state
+    attended[...] = state
     mean = jnp.mean(state * state, axis=1, keepdims=True)
-    rows[:, :width] = (state * lax.rsqrt(mean + norm_eps) * gain[...]).astype(
+    rows[:, :width] = (state * lax.rsqrt(mean + norm_eps) * gain[...][None]).astype(
         jnp.bfloat16
     )
-    experts_kernel(rows, *weights, mixture_out, hist_out, *expert_refs)
+    experts_kernel(rows, *weights, mixture, hist_out, *expert_refs)
+    total = jnp.sum(levels[...].astype(jnp.float32), axis=1, keepdims=True)
+    layer_out[...] = attended[...] + mixture[...] / total
 
 
 def run_layer(attend_in, uv_weight, weight, row_in, gate, up, down, part_a=2048):
@@ -897,12 +899,12 @@
         functools.partial(layer_kernel, part_a, len(attend_refs)),
         out_shape=(
             jax.ShapeDtypeStruct((TOK, width), jnp.float32),
-            jax.ShapeDtypeStruct((TOK, width), jnp.float32),
             jax.ShapeDtypeStruct((8, 2 * N_EXPERTS), jnp.float32),
         ),
         in_specs=[vmem] * 5 + [hbm] * 2 + [vmem] * 5 + [hbm] * 3,
-        out_specs=(vmem, vmem, vmem),
+        out_specs=(vmem, vmem),
         scratch_shapes=[
+            pltpu.VMEM((TOK, width), jnp.float32),
             pltpu.VMEM((TOK, width), jnp.float32),
             pltpu.VMEM((TOK, width + 4 * N_EXPERTS), jnp.bfloat16),
             *attend_refs,
@@ -933,17 +935,16 @@
     down_weight,
 ):
     block_len = q_nope.shape[0]
-    stream_state, mixture, hist = run_layer(
+    layer_out, hist = run_layer(
         (q_nope, q_rope, latent, k_rope.T, doc_ids.reshape(1, block_len)),
         uv_weight,
         out_weight,
-        (residual_in, norm_gain[None], expert_ids, gate_levels, bin_ids),
+        (residual_in, norm_gain, expert_ids, gate_levels, bin_ids),
         gate_weight[0],
         up_weight[0],
         down_weight[0],
     )
-    scale = 1.0 / jnp.sum(gate_levels.astype(jnp.float32), axis=1, keepdims=True)
-    layer_out = (stream_state + mixture * scale).astype(jnp.bfloat16)
+    layer_out = layer_out.astype(jnp.bfloat16)
     histogram = hist[:, : NBINS // 32].reshape(1, NBINS // N_CTX)
     return (layer_out, histogram)
 

time: 153 us -> 152 us (level)
  no operation moved by 1% of the time
where the time goes in v8:
time: 152 us; the launch traced here: 150 us
  Pallas kernels  146 us (96%)
  other arithmetic  1.53 us (1%)
    pallas_call x1, Pallas kernels, run_layer(): pl.pallas_call(functools.partial(layer_kernel, part_a, len(attend_refs)),...  146 us

profile of v8, /device:TPU:1, one launch (start us, length us, event | category | flops | bytes accessed | tf_op | source)
XLA Modules:
  0.0 149.5 jit_solution(9306570724676585014)
XLA Ops:
  0.6 146.0 %layer.1 = (f32[8,3584]{1,0:T(8,128)}, f32[8,128]{1,0:T(8,128)}) custom-call(bf16[512,2,512]{2,1,0:T(2,128)(2,1)} %refs_0_.1, bf16[512,128]{1,0:T(8,128)(2,1)} %refs_1_.1, bf16[512,512]{1,0:T(8,128)(2,1)} %refs_2_.1, bf16[64,512]{1,0:T(8,128)(2,1)} %bitcast.9, s32[1,512]{1,0:T(1,128)} %bitcast.11, bf16[2,512,128]{2,1,0:T(8,128)(2,1)} %refs_5_.1, ...), custom_call_target="tpu_custom_call" | custom-call | tf_op jit(solution)/shard_map/layer/pallas_call | solution.py:898
  146.7 1.5 %convert_element_type.3 = bf16[8,3584]{1,0:T(8,128)(2,1)} convert(f32[8,3584]{1,0:T(8,128)} %get-tuple-element.4) | non-fusion elementwise | flops 28672 | bytes 172032 | tf_op jit(solution)/shard_map/convert_element_type | solution.py:947
  148.2 1.3 reshape.11

commit v9 on v8

--- a/solution.py
+++ b/solution.py
@@ -93,6 +93,7 @@
     denominator,
     accum,
     values_ref,
+    partial_ref,
     a_first,
     a_slots,
     b_first,
@@ -307,15 +308,20 @@
             .reshape(NZ, NX, NY * TOK, VDIM)
         )
 
+    def project(start, stop):
+        rows = values_ref[...].reshape(block_len, heads * VDIM)
+        for first in range(start, stop, 512):
+            shape = (NZ, NX, NY * TOK, 512)
+            product = mm(rows, weight_ref[:, first : first + 512])
+            partial_ref[:, :, :, first : first + 512] = product.reshape(shape)
+
     def a_own(way, sub, chunk):
-        rows = values_ref[chunk].reshape(NX * NY * TOK, values_ref.shape[3])
         start = (way * SUBS + sub) * wide_a
-        return mm(rows, weight_ref[:, start : start + wide_a])
+        return partial_ref[chunk, :, :, start : start + wide_a].reshape(-1, wide_a)
 
     def b_own(way, sub, chunk):
-        rows = values_ref[:, chunk].reshape(NZ * NY * TOK, values_ref.shape[3])
         start = part_a + (way * SUBS + sub) * wide_b
-        return mm(rows, weight_ref[:, start : start + wide_b])
+        return partial_ref[:, chunk, :, start : start + wide_b].reshape(-1, wide_b)
 
     a_flight, b_flight, pushes = {}, {}, []
 
@@ -417,7 +423,9 @@
                 )
             )
 
+    project(0, part_a)
     a_step(0)
+    project(part_a, width)
     b_step(0)
     a_step(1)
     a_step(2)
@@ -473,6 +481,7 @@
             pltpu.VMEM((heads, rows, 128), jnp.float32),
             pltpu.VMEM((heads, rows, lat), jnp.float32),
             pltpu.VMEM((NZ, NX, NY * TOK, heads * VDIM), bf16),
+            pltpu.VMEM((NZ, NX, NY * TOK, width), jnp.float32),
             pltpu.VMEM((2, SUBS, NQ * TOK, wide_a), bf16),
             pltpu.VMEM((2, SUBS, NZ - 1, NQ * TOK, wide_a), bf16),
             pltpu.VMEM((2, SUBS, NR * TOK, wide_b), bf16),

time: 152 us -> 150 us (0.987)
  Pallas kernels: 146 us -> 143 us
    pallas_call x1, Pallas kernels: 146 us -> 143 us  [run_layer(): pl.pallas_call(functools.partial(layer_kernel, part_a, len(attend_refs)),...]
where the time goes in v9:
time: 150 us; the launch traced here: 147 us
  Pallas kernels  143 us (95%)
  other arithmetic  1.53 us (1%)
    pallas_call x1, Pallas kernels, run_layer(): pl.pallas_call(functools.partial(layer_kernel, part_a, len(attend_refs)),...  143 us

profile of v9, /device:TPU:1, one launch (start us, length us, event | category | flops | bytes accessed | tf_op | source)
XLA Modules:
  0.0 147.0 jit_solution(7873385545315080483)
XLA Ops:
  0.6 143.5 %layer.1 = (f32[8,3584]{1,0:T(8,128)}, f32[8,128]{1,0:T(8,128)}) custom-call(bf16[512,2,512]{2,1,0:T(2,128)(2,1)} %refs_0_.1, bf16[512,128]{1,0:T(8,128)(2,1)} %refs_1_.1, bf16[512,512]{1,0:T(8,128)(2,1)} %refs_2_.1, bf16[64,512]{1,0:T(8,128)(2,1)} %bitcast.9, s32[1,512]{1,0:T(1,128)} %bitcast.11, bf16[2,512,128]{2,1,0:T(8,128)(2,1)} %refs_5_.1, ...), custom_call_target="tpu_custom_call" | custom-call | tf_op jit(solution)/shard_map/layer/pallas_call | solution.py:907
  144.1 1.5 %convert_element_type.3 = bf16[8,3584]{1,0:T(8,128)(2,1)} convert(f32[8,3584]{1,0:T(8,128)} %get-tuple-element.4) | non-fusion elementwise | flops 28672 | bytes 172032 | tf_op jit(solution)/shard_map/convert_element_type | solution.py:956
  145.7 1.3 reshape.11
